TPU v7x, 256 devices: a whole 4x4x8 slice. The times are simulated.
256 devices in a mesh: filt: 16 (over y, z_hi), chan: 4 (over x), tile: 4 (over z_lo, core).
Axes of the slice: x: 4, y: 4, z: 8 (z_hi: 4, z_lo: 2; z = z_hi * 2 + z_lo), core: 2. Of those that a mesh axis runs over, the one named last changes fastest.
Arguments:
- saved_input: bfloat16 [256, 48, 2048], P('tile', 'filt', 'chan'), may hold values from -1.5 to 1.5
- upstream: bfloat16 [256, 48, 2048], P('tile', None, 'filt'), may hold values from -4 to 4
- kernel: bfloat16 [3, 3, 2048, 2048], P(None, None, 'chan', 'filt'), may hold values from -0.046875 to 0.046875
Outputs:
- input_grad: bfloat16 [256, 48, 2048], P('tile', 'filt', 'chan')
- kernel_grad: float32 [3, 3, 2048, 2048], P(None, None, ('chan', 'tile'), 'filt')
All inputs are finite; a program needn't handle non-finite values.
Results may differ from a plain program's by a relative error of at most 0.014.
Values may be sent and summed in bfloat16 or wider, within the bound.
A program may use at most 128 MiB of HBM per device.

v0:
```python
import jax
import jax.numpy as jnp
from jax import lax
from jax.sharding import PartitionSpec as P


def padded_2(value, sides, width):
    for axis, dim in sides:
        count, length = (lax.axis_size(axis), value.shape[dim])
        up = [(i, (i + 1) % count) for i in range(count - 1)]
        down = [(j, i) for i, j in up]
        last = lax.slice_in_dim(value, length - width, length, axis=dim)
        leading = lax.slice_in_dim(value, 0, width, axis=dim)
        before = lax.ppermute(last, axis, up)
        after = lax.ppermute(leading, axis, down)
        value = jnp.concatenate([before, value, after], axis=dim)
    return value


def shifted_blocks(padded, height, breadth, direction):
    pieces = []
    for step_row in (-1, 0, 1):
        for step_col in (-1, 0, 1):
            top = 1 + direction * step_row
            left = 1 + direction * step_col
            pieces.append(padded[top : top + height, left : left + breadth])
    return jnp.concatenate(pieces, axis=2)


def per_device(saved_input, upstream, kernel):
    height, breadth, out_width = upstream.shape
    in_width = kernel.shape[2]
    active = jnp.maximum(saved_input, jnp.zeros((), jnp.bfloat16))
    gathered = lax.all_gather(active, "filt", axis=1, tiled=True)
    rimmed_grad = padded_2(upstream, (("tile", 0),), 1)
    padded_grad = jnp.pad(rimmed_grad, ((0, 0), (1, 1), (0, 0)))
    stacked_grad = shifted_blocks(padded_grad, height, breadth, -1).reshape(
        height * breadth, 9 * out_width
    )
    kernel_flat = jnp.transpose(kernel.reshape(9, in_width, out_width), (0, 2, 1)).reshape(
        9 * out_width, in_width
    )
    partial_value = jnp.dot(stacked_grad, kernel_flat, preferred_element_type=jnp.float32).reshape(
        height, breadth, in_width
    )
    summed = lax.psum_scatter(
        partial_value.astype(jnp.bfloat16), "filt", scatter_dimension=1, tiled=True
    ).astype(jnp.float32)
    masked = jnp.where(saved_input > 0, summed, jnp.zeros((), jnp.float32))
    input_grad = masked.astype(jnp.bfloat16)
    rimmed_input = padded_2(gathered, (("tile", 0),), 1)
    padded_input = jnp.pad(rimmed_input, ((0, 0), (1, 1), (0, 0)))
    stacked_input = shifted_blocks(padded_input, height, breadth, 1).reshape(
        height * breadth, 9 * in_width
    )
    kernel_part = jnp.dot(
        stacked_input.T,
        upstream.reshape(height * breadth, out_width),
        preferred_element_type=jnp.float32,
    )
    kernel_part = kernel_part.reshape(3, 3, in_width, out_width)
    kernel_grad = lax.psum_scatter(
        kernel_part.astype(jnp.bfloat16), "tile", scatter_dimension=2, tiled=True
    ).astype(jnp.float32)
    return (input_grad, kernel_grad)


def solution(mesh):
    placed = (P("tile", "filt", "chan"), P("tile", None, "filt"), P(None, None, "chan", "filt"))
    return jax.shard_map(
        per_device,
        mesh=mesh,
        in_specs=placed,
        out_specs=(P("tile", "filt", "chan"), P(None, None, ("chan", "tile"), "filt")),
        check_vma=False,
    )
```

profile of v0, /device:TPU:1, one launch (start us, length us, event | category | flops | bytes accessed | tf_op | source)
XLA Modules:
  0.0 209.6 jit_solution(4565965917224521228)
XLA Ops:
  7.2 0.0 copy-start.1
  7.2 0.0 all-gather.2.cloned.1.call-start
  7.2 1.7 broadcast_maximum_fusion
  8.9 0.0 all-gather.2.cloned.1.call-update
  8.9 0.0 reduce-scatter.3.cloned.1.call-start
  9.0 0.7 fusion.17
  9.7 4.9 %collective-permute-start = (bf16[1,48,128]{2,1,0:T(8,128)(2,1)S(1)}, bf16[1,48,128]{2,1,0:T(8,128)(2,1)S(1)}, u32[]{:S(2)}, u32[]{:S(2)}) collective-permute-start(bf16[1,48,128]{2,1,0:T(8,128)(2,1)S(1)} %get-tuple-element.6), channel_id=1, source_target_pairs={{0,1},{1,2},{2,3},{4,5},{5,6},{6,7},{8,9},{9,10},{10,11},{12,13},{... | collective-permute-start | bytes 36872 | tf_op jit(solution)/shard_map/ppermute | solution.py:14
  14.6 1.9 collective-permute-start.1
  16.6 1.6 copy.12
  18.1 0.0 collective-permute-done
  18.2 1.5 collective-permute-done.1
  19.6 1.5 fusion.13
  21.2 0.3 slice_dynamic-update-slice_fusion.11
  21.4 0.0 copy-done.1
  21.5 0.2 fusion.15
  21.6 0.2 slice_dynamic-update-slice_fusion.10
  21.8 0.4 slice_dynamic-update-slice_fusion.9
  22.2 0.2 constant_dynamic-update-slice_fusion
  22.4 0.2 slice_dynamic-update-slice_fusion.8
  22.6 0.4 slice_dynamic-update-slice_fusion.7
  23.0 0.2 fusion.14
  23.2 0.2 slice_dynamic-update-slice_fusion.6
  23.4 4.5 %convolution_convert_fusion = bf16[64,48,512]{2,1,0:T(8,128)(2,1)S(1)} fusion(bf16[64,48,1152]{2,1,0:T(8,128)(2,1)S(1)} %slice_dynamic-update-slice_fusion.6, bf16[1152,512,1]{1,0,2:T(8,128)(2,1)S(1)} %bitcast.23), kind=kOutput, calls=%fused_computation.20 | convolution fusion | flops 3625451520 | bytes 11403264 | tf_op jit(solution)/shard_map/dot_general | solution.py:43
  27.9 3.4 %copy.13 = bf16[64,48,512]{2,0,1:T(8,128)(2,1)} copy(bf16[64,48,512]{2,1,0:T(8,128)(2,1)S(1)} %convolution_convert_fusion) | data formatting | bytes 6291456 | tf_op jit(solution)/shard_map/convert_element_type | solution.py:47
  31.3 0.0 reduce-scatter.3.cloned.1.call-update
  31.3 0.0 reduce-scatter.5.cloned.1.call-start
  31.4 50.9 %all-gather.2.cloned.1.call-done = bf16[64,48,512]{2,0,1:T(8,128)(2,1)} async-done(((bf16[64,3,512]{2,0,1:T(8,128)(2,1)}), bf16[64,48,512]{2,0,1:T(8,128)(2,1)}) %all-gather.2.cloned.1.call-update) | async-done | bytes 3145744 | tf_op jit(solution)/shard_map/all_gather | solution.py:34
  82.3 3.6 %copy.14 = bf16[64,48,512]{2,1,0:T(8,128)(2,1)S(1)} copy(bf16[64,48,512]{2,0,1:T(8,128)(2,1)} %all-gather.2.cloned.1.call-done) | data formatting | bytes 6291456 | tf_op jit(solution)/shard_map/all_gather | solution.py:34
  85.9 1.9 collective-permute-start.2
  87.9 2.6 %collective-permute-start.3 = (bf16[1,48,512]{2,1,0:T(8,128)(2,1)S(1)}, bf16[1,48,512]{2,1,0:T(8,128)(2,1)S(1)}, u32[]{:S(2)}, u32[]{:S(2)}) collective-permute-start(bf16[1,48,512]{2,1,0:T(8,128)(2,1)S(1)} %get-tuple-element.5), channel_id=1, source_target_pairs={{1,0},{2,1},{3,2},{5,4},{6,5},{7,6},{9,8},{10,9},{11,10},{13,12},{... | collective-permute-start | bytes 147464 | tf_op jit(solution)/shard_map/ppermute | solution.py:15
  90.5 0.0 collective-permute-done.2
  90.5 2.8 %collective-permute-done.3 = bf16[1,48,512]{2,1,0:T(8,128)(2,1)S(1)} collective-permute-done((bf16[1,48,512]{2,1,0:T(8,128)(2,1)S(1)}, bf16[1,48,512]{2,1,0:T(8,128)(2,1)S(1)}, u32[]{:S(2)}, u32[]{:S(2)}) %collective-permute-start.3) | collective-permute-done | bytes 49184 | tf_op jit(solution)/shard_map/ppermute | solution.py:15
  93.3 1.9 fusion.5
  95.2 0.4 slice_dynamic-update-slice_fusion.5
  95.7 0.2 fusion.7
  95.9 1.6 slice_dynamic-update-slice_fusion.4
  97.5 0.4 slice_dynamic-update-slice_fusion.3
  98.0 3.6 %constant_dynamic-update-slice_fusion.1 = bf16[64,48,4608]{2,1,0:T(8,128)(2,1)S(1)} fusion(bf16[64,48,4608]{2,1,0:T(8,128)(2,1)S(1)} %slice_dynamic-update-slice_fusion.3, bf16[64,48,512]{2,0,1:T(8,128)(2,1)} %all-gather.2.cloned.1.call-done), kind=kLoop, calls=%fused_computation.41 | loop fusion | bytes 6291456
  101.6 1.6 slice_dynamic-update-slice_fusion.2
  103.3 0.4 slice_dynamic-update-slice_fusion.1
  103.8 0.2 fusion.6
  104.0 1.6 slice_dynamic-update-slice_fusion
  105.6 0.0 copy-start
  105.6 9.7 %copy-done = bf16[64,48,4608]{2,1,0:T(8,128)(2,1)} copy-done((bf16[64,48,4608]{2,1,0:T(8,128)(2,1)}, bf16[64,48,4608]{2,1,0:T(8,128)(2,1)S(1)}, u32[]{:S(2)}) %copy-start) | copy-done | bytes 28311576
  115.3 36.7 %copy.20 = bf16[4608,3072]{1,0:T(8,128)(2,1)} copy(bf16[4608,3072]{0,1:T(8,128)(2,1)} %bitcast.19) | data formatting | bytes 56623104 | tf_op jit(solution)/shard_map/dot_general | solution.py:56
  152.0 0.0 copy-start.2
  152.0 14.0 %convolution_convert_fusion.1 = bf16[3,3,512,128]{3,2,1,0:T(8,128)(2,1)} fusion(bf16[3,3,512,3072]{3,2,1,0:T(8,128)(2,1)} %bitcast.20, bf16[3072,128,1,1]{1,0,3,2:T(8,128)(2,1)S(1)} %bitcast.21), kind=kOutput, calls=%fused_computation.22 | convolution fusion | flops 3624468480 | bytes 30277632 | tf_op jit(solution)/shard_map/dot_general | solution.py:56
  166.0 0.0 reduce-scatter.5.cloned.1.call-update
  166.1 9.8 %reduce-scatter.3.cloned.1.call-done = bf16[64,3,512]{2,0,1:T(8,128)(2,1)} async-done(((bf16[64,48,512]{2,0,1:T(8,128)(2,1)}), bf16[64,3,512]{2,0,1:T(8,128)(2,1)}) %reduce-scatter.3.cloned.1.call-update) | async-done | bytes 196624 | tf_op jit(solution)/shard_map/reduce_scatter | solution.py:46
  175.9 0.0 copy-done.2
  175.9 1.7 select_convert_fusion
  177.5 23.7 %reduce-scatter.5.cloned.1.call-done = bf16[3,3,128,128]{3,2,1,0:T(8,128)(2,1)} async-done(((bf16[3,3,512,128]{3,2,1,0:T(8,128)(2,1)}), bf16[3,3,128,128]{3,2,1,0:T(8,128)(2,1)}) %reduce-scatter.5.cloned.1.call-update) | async-done | bytes 294928 | tf_op jit(solution)/shard_map/reduce_scatter | solution.py:62
  201.3 1.8 convert_element_type.23
  (1 shorter events, 0.0 us)
Async XLA Ops:
  7.2 14.3 %copy-start.1 = (bf16[64,48,128]{2,1,0:T(8,128)(2,1)S(1)}, bf16[64,48,128]{2,1,0:T(8,128)(2,1)}, u32[]{:S(2)}) copy-start(bf16[64,48,128]{2,1,0:T(8,128)(2,1)} %param.4) | copy-start | bytes 2359300
  7.2 75.1 %all-gather.2.cloned.1.call-start = ((), (), s32[]{:S(2)}) async-start(), calls=%async_computation.3 | async-start | bytes 3342336 | tf_op jit(solution)/shard_map/all_gather | solution.py:34
  8.9 166.9 %reduce-scatter.3.cloned.1.call-start = ((), (), s32[]{:S(2)}) async-start(), calls=%async_computation.2 | async-start | bytes 3342336 | tf_op jit(solution)/shard_map/reduce_scatter | solution.py:46
  9.7 8.4 %collective-permute-start = (bf16[1,48,128]{2,1,0:T(8,128)(2,1)S(1)}, bf16[1,48,128]{2,1,0:T(8,128)(2,1)S(1)}, u32[]{:S(2)}, u32[]{:S(2)}) collective-permute-start(bf16[1,48,128]{2,1,0:T(8,128)(2,1)S(1)} %get-tuple-element.6), channel_id=1, source_target_pairs={{0,1},{1,2},{2,3},{4,5},{5,6},{6,7},{8,9},{9,10},{10,11},{12,13},{... | collective-permute-start | bytes 36872 | tf_op jit(solution)/shard_map/ppermute | solution.py:14
  14.6 5.0 %collective-permute-start.1 = (bf16[1,48,128]{2,1,0:T(8,128)(2,1)S(1)}, bf16[1,48,128]{2,1,0:T(8,128)(2,1)S(1)}, u32[]{:S(2)}, u32[]{:S(2)}) collective-permute-start(bf16[1,48,128]{2,1,0:T(8,128)(2,1)S(1)} %get-tuple-element.7), channel_id=1, source_target_pairs={{1,0},{2,1},{3,2},{5,4},{6,5},{7,6},{9,8},{10,9},{11,10},{13,12},{... | collective-permute-start | bytes 36872 | tf_op jit(solution)/shard_map/ppermute | solution.py:15
  31.3 169.9 %reduce-scatter.5.cloned.1.call-start = ((), (), s32[]{:S(2)}) async-start(), calls=%async_computation.4 | async-start | bytes 1474560 | tf_op jit(solution)/shard_map/reduce_scatter | solution.py:62
  85.9 4.5 %collective-permute-start.2 = (bf16[1,48,512]{2,1,0:T(8,128)(2,1)S(1)}, bf16[1,48,512]{2,1,0:T(8,128)(2,1)S(1)}, u32[]{:S(2)}, u32[]{:S(2)}) collective-permute-start(bf16[1,48,512]{2,1,0:T(8,128)(2,1)S(1)} %get-tuple-element.4), channel_id=1, source_target_pairs={{0,1},{1,2},{2,3},{4,5},{5,6},{6,7},{8,9},{9,10},{10,11},{12,13},{... | collective-permute-start | bytes 147464 | tf_op jit(solution)/shard_map/ppermute | solution.py:14
  87.9 5.4 %collective-permute-start.3 = (bf16[1,48,512]{2,1,0:T(8,128)(2,1)S(1)}, bf16[1,48,512]{2,1,0:T(8,128)(2,1)S(1)}, u32[]{:S(2)}, u32[]{:S(2)}) collective-permute-start(bf16[1,48,512]{2,1,0:T(8,128)(2,1)S(1)} %get-tuple-element.5), channel_id=1, source_target_pairs={{1,0},{2,1},{3,2},{5,4},{6,5},{7,6},{9,8},{10,9},{11,10},{13,12},{... | collective-permute-start | bytes 147464 | tf_op jit(solution)/shard_map/ppermute | solution.py:15
  105.6 9.7 %copy-start = (bf16[64,48,4608]{2,1,0:T(8,128)(2,1)}, bf16[64,48,4608]{2,1,0:T(8,128)(2,1)S(1)}, u32[]{:S(2)}) copy-start(bf16[64,48,4608]{2,1,0:T(8,128)(2,1)S(1)} %slice_dynamic-update-slice_fusion) | copy-start | bytes 84934656
  152.0 23.8 %copy-start.2 = (bf16[64,3,512]{2,0,1:T(8,128)(2,1)S(1)}, bf16[64,3,512]{2,0,1:T(8,128)(2,1)}, u32[]{:S(2)}) copy-start(bf16[64,3,512]{2,0,1:T(8,128)(2,1)} %param.3) | copy-start | bytes 589828
Sparse Core Ops, SparseCore 0:
  11.0 71.2 all-gather.1
  85.9 89.9 reduce-scatter.2
  178.4 22.7 reduce-scatter.4
where the time goes:
time: 211 us; the launch traced here: 210 us
  waiting for transfers between devices  88.8 us (42%)
  local copies, waits for them, and re-layouts  67.5 us (32%)
  matrix products  18.5 us (9%)
  between operations  14 us (7%)
  starting transfers between devices  11.5 us (5%)
  other arithmetic  9.42 us (4%)
    all_gather x1, waiting for transfers between devices, per_device(): gathered = lax.all_gather(active, 'filt', axis=1, tiled=True)  50.9 us
    dot_general x1, local copies, waits for them, and re-layouts, per_device(): jnp.dot(stacked_input.T, upstream.reshape(height * breadth, out_width), p...  36.7 us
    reduce_scatter x1, waiting for transfers between devices, per_device(): lax.psum_scatter(kernel_part.astype(jnp.bfloat16), 'tile', scatter_dimens...  23.7 us
    unnamed x18, local copies, waits for them, and re-layouts  19.6 us
    dot_general x1, matrix products, per_device(): jnp.dot(stacked_input.T, upstream.reshape(height * breadth, out_width), p...  14 us
    reduce_scatter x1, waiting for transfers between devices, per_device(): lax.psum_scatter(partial_value.astype(jnp.bfloat16), 'filt', scatter_dime...  9.81 us
    ppermute x2, starting transfers between devices, padded_2(): before = lax.ppermute(last, axis, up)  6.83 us
    ppermute x2, starting transfers between devices, padded_2(): after = lax.ppermute(leading, axis, down)  4.51 us
  transfers between devices with their start and end apart: 7, of which 5 were waited for; matrix products, arithmetic and copies ran while one was open for 39% of the time, Pallas kernels for 0%

commit v1 on v0

v1 whole, which is shorter than its diff:
```python
import jax
import jax.numpy as jnp
from jax import lax
from jax.experimental import pallas as pl
from jax.experimental.pallas import tpu as pltpu
from jax.sharding import PartitionSpec as P

BF16, F32 = jnp.bfloat16, jnp.float32
NY, NZ = 4, 4
UP, DOWN = 0, 1
SIGN = (1, -1)
NEAR = (1, 3)

Z1, Z2 = (0, 1), (2, 3)
Y1 = ((4, 5, 6, 7), (8, 9, 10, 11))
Y2 = ((12, 13, 14, 15), (16, 17, 18, 19))
FAR = ((20, 21), (22, 23))
NR = ((24, 25, 26, 27), (28, 29, 30, 31))
ZF, ZN = (32, 33), (34, 35)
WC, WZ = (36, 37), 38
HALO = (39, 40)
MESSAGES = 41

FAR_BLOCKS = ((2, 1), (3, 0))


def kernel(
    x_ref, u_ref, k_ref, gi_ref, gk_ref,
    kc, uf, s_buf, a_buf, p_buf, far_in, near_in, zfar_in, znear_in,
    wacc, at, wb, wc_in, wz_out, wz_in, halo, ssem, rsem, lsem,
):
    rows, cols, width = u_ref.shape
    chunk = x_ref.shape[0]
    half = chunk // 2
    own_cols = chunk // rows
    group_cols = NZ * own_cols
    taps = 3 * width
    filt, tile = lax.axis_index("filt"), lax.axis_index("tile")
    y, z = lax.div(filt, NZ), lax.rem(filt, NZ)
    lo, core = lax.div(tile, 2), lax.rem(tile, 2)

    def zed(step):
        return lax.rem(z + step, NZ)

    def ycoord(step):
        return lax.rem(y + step, NY)

    def at_y(direction):
        return {"filt": ycoord(NEAR[direction]) * NZ + z}

    def at_z(direction):
        return {"filt": y * NZ + zed(NEAR[direction])}

    def send(number, src, dst, peer):
        return pltpu.make_async_remote_copy(
            src_ref=src, dst_ref=dst, send_sem=ssem.at[number], recv_sem=rsem.at[number],
            device_id=peer, device_id_type=pl.DeviceIdType.MESH,
        )

    started = []

    def start(copy):
        copy.start()
        started.append(copy)

    other_core = {"tile": lo * 2 + 1 - core}
    other_lo = {"tile": (1 - lo) * 2 + core}
    cross = {"tile": (1 - lo) * 2 + 1 - core}

    barrier = pltpu.get_barrier_semaphore()
    peers = [at_y(UP), at_y(DOWN), at_z(UP), at_z(DOWN), other_core, other_lo, cross]
    for peer in peers:
        pl.semaphore_signal(barrier, inc=1, device_id=peer, device_id_type=pl.DeviceIdType.MESH)
    pl.semaphore_wait(barrier, len(peers))

    def halves(direction):
        return pl.ds(direction * half, half)

    def z1(d):
        return send(Z1[d], x_ref, a_buf.at[0, z], at_z(d))

    def z2(d):
        slot = a_buf.at[0, zed(NEAR[1 - d]), halves(d)]
        return send(Z2[d], slot, slot, at_z(d))

    def y1(d, b):
        src = x_ref if b == 0 else a_buf.at[0, zed(b)]
        return send(Y1[d][b], src, a_buf.at[NEAR[1 - d], zed(b)], at_y(d))

    def y2(d, b):
        return send(
            Y2[d][b], a_buf.at[NEAR[1 - d], zed(b), halves(d)], a_buf.at[2, zed(b), halves(d)], at_y(d)
        )

    def far(d, k):
        return send(FAR[d][k], p_buf.at[2, zed(FAR_BLOCKS[d][k])], far_in.at[d, k], at_y(d))

    def near(d, b):
        return send(NR[d][b], p_buf.at[NEAR[d], zed(b)], near_in.at[d, b], at_y(d))

    def zfar(d):
        return send(ZF[d], p_buf.at[0, zed(2), halves(d)], zfar_in.at[d], at_z(d))

    def znear(d):
        return send(ZN[d], p_buf.at[0, zed(NEAR[d])], znear_in.at[d], at_z(d))

    def wcore(k):
        return send(WC[k], wb.at[2 * k + 1 - core], wc_in.at[k], other_core)

    def wlo():
        return send(WZ, wz_out, wz_in, other_lo)

    def halo_down():
        return send(HALO[0], u_ref.at[0], halo.at[1], {"tile": tile - 1})

    def halo_up():
        return send(HALO[1], u_ref.at[rows - 1], halo.at[0], {"tile": tile + 1})

    first, last = tile == 0, tile == 3

    for d in (UP, DOWN):
        start(z1(d))
        start(y1(d, 0))

    @pl.when(jnp.logical_not(first))
    def _():
        halo_down().start()

    @pl.when(jnp.logical_not(last))
    def _():
        halo_up().start()

    own = pltpu.make_async_copy(x_ref, a_buf.at[0, z], lsem.at[9])
    own.start()
    weights = []
    for si in range(3):
        for ri in range(3):
            place = si * 3 + ri
            copy = pltpu.make_async_copy(
                k_ref.at[ri * 3 + si], kc.at[:, pl.ds(place * width, width)], lsem.at[place]
            )
            copy.start()
            weights.append(copy)

    @pl.loop(0, rows)
    def _(i):
        uf[pl.ds(pl.multiple_of((i + 1) * cols, 8), cols), :] = u_ref[i].astype(F32)

    s_buf[1, :, 2 * taps :] = jnp.zeros((rows, taps), BF16)
    s_buf[cols, :, :taps] = jnp.zeros((rows, taps), BF16)

    @pl.when(first)
    def _():
        uf[:cols, :] = jnp.zeros((cols, width), F32)

    @pl.when(jnp.logical_not(first))
    def _():
        halo_up().wait_recv()
        uf[:cols, :] = halo[0].astype(F32)

    bottom = (rows + 1) * cols

    @pl.when(last)
    def _():
        uf[bottom:, :] = jnp.zeros((cols, width), F32)

    @pl.when(jnp.logical_not(last))
    def _():
        halo_down().wait_recv()
        uf[bottom:, :] = halo[1].astype(F32)

    @pl.loop(0, cols)
    def _(j):
        for ri in range(3):
            value = uf[pl.ds((2 - ri) * cols + j, rows, stride=cols), :].astype(BF16)
            for si in range(3):
                s_buf[j + si, :, pl.ds(si * taps + ri * width, width)] = value

    for copy in weights:
        copy.wait()

    def stacked(a):
        block = s_buf[pl.ds(ycoord(a) * group_cols + 1, group_cols)]
        return block.reshape(NZ * chunk, 3 * taps)

    def dgrad(a):
        part = lax.dot_general(
            stacked(a), kc[...], (((1,), (1,)), ((), ())), preferred_element_type=F32
        )
        p_buf[a] = part.astype(BF16).reshape(NZ, chunk, part.shape[1])

    def wgrad(a):
        chunks = a_buf[a].reshape(NZ * chunk, a_buf.shape[3])
        at[...] = jnp.maximum(chunks, jnp.zeros((), BF16)).T
        part = jnp.dot(at[...], stacked(a), preferred_element_type=F32).reshape(wacc.shape)
        if a == 0:
            wacc[...] = part
        else:
            wacc[...] += part

    def add_far(d, k):
        slot = (NEAR[d], zed(FAR_BLOCKS[d][k]))
        far(d, k).wait_recv()
        p_buf[slot] = (p_buf[slot].astype(F32) + far_in[d, k].astype(F32)).astype(BF16)

    def near_sum(b):
        near(UP, b).wait_recv()
        near(DOWN, b).wait_recv()
        return p_buf[0, zed(b)].astype(F32) + near_in[UP, b].astype(F32) + near_in[DOWN, b].astype(F32)

    dgrad(2)
    for k in (0, 1):
        for d in (UP, DOWN):
            start(far(d, k))
    dgrad(1)
    dgrad(3)
    for d in (UP, DOWN):
        z1(d).wait_recv()
        b = NEAR[1 - d]
        start(z2(d))
        start(y1(UP, b))
        start(y1(DOWN, b))
    for d in (UP, DOWN):
        y1(d, 0).wait_recv()
        start(y2(d, 0))
    dgrad(0)
    add_far(UP, 0)
    start(near(UP, 2))
    start(near(DOWN, 2))
    for d in (UP, DOWN):
        z2(d).wait_recv()
    for d in (UP, DOWN):
        start(y1(d, 2))
    own.wait()
    wgrad(0)
    for b in (3, 1):
        for d in (UP, DOWN):
            y1(d, b).wait_recv()
            start(y2(d, b))
    for d in (UP, DOWN):
        y1(d, 2).wait_recv()
        start(y2(d, 2))
    add_far(UP, 1)
    start(near(UP, 1))
    start(near(DOWN, 1))
    add_far(DOWN, 0)
    start(near(UP, 3))
    start(near(DOWN, 3))
    add_far(DOWN, 1)
    start(near(UP, 0))
    start(near(DOWN, 0))
    wgrad(3)
    wgrad(1)
    p_buf[0, zed(2)] = near_sum(2).astype(BF16)
    for d in (UP, DOWN):
        start(zfar(d))
    for b in range(NZ):
        for d in (UP, DOWN):
            y2(d, b).wait_recv()
    wgrad(2)
    wb[...] = wacc[...].astype(BF16)
    for k in (0, 1):
        start(wcore(k))
    for d in (UP, DOWN):
        b = NEAR[d]
        total = near_sum(b)
        zfar(d).wait_recv()
        p_buf[0, zed(b)] = total.astype(BF16)
        p_buf[0, zed(b), halves(d)] = (
            total[d * half : (d + 1) * half] + zfar_in[d].astype(F32)
        ).astype(BF16)
        start(znear(d))
    for k in (0, 1):
        wcore(k).wait_recv()
    wz_out[...] = (wacc[2 * (1 - lo) + core] + wc_in[1 - lo].astype(F32)).astype(BF16)
    start(wlo())
    total = near_sum(0)
    for d in (UP, DOWN):
        znear(d).wait_recv()
    total += znear_in[UP].astype(F32) + znear_in[DOWN].astype(F32)
    gi_ref[...] = jnp.where(x_ref[...] > 0, total, 0.0).astype(BF16)
    wlo().wait_recv()
    grad = wacc[tile] + wc_in[lo].astype(F32) + wz_in[...].astype(F32)
    for si in range(3):
        for ri in range(3):
            place = (si * 3 + ri) * width
            gk_ref[ri * 3 + si] = grad[:, place : place + width]
    for copy in started:
        copy.wait_send()

    @pl.when(jnp.logical_not(first))
    def _():
        halo_down().wait_send()

    @pl.when(jnp.logical_not(last))
    def _():
        halo_up().wait_send()


def per_device(saved_input, upstream, weights):
    rows, cols, width = upstream.shape
    own_cols, channels = saved_input.shape[1], saved_input.shape[2]
    chunk = own_cols * rows
    half = chunk // 2
    x = jnp.transpose(saved_input, (1, 0, 2)).reshape(chunk, channels)
    vmem = pl.BlockSpec(memory_space=pltpu.VMEM)
    block = channels // 4
    gi, gk = pl.pallas_call(
        kernel,
        name="conv_backward",
        out_shape=(
            jax.ShapeDtypeStruct((chunk, channels), BF16),
            jax.ShapeDtypeStruct((9, block, width), F32),
        ),
        in_specs=[vmem, vmem, pl.BlockSpec(memory_space=pl.ANY)],
        out_specs=(vmem, vmem),
        scratch_shapes=[
            pltpu.VMEM((channels, 9 * width), BF16),
            pltpu.VMEM(((rows + 2) * cols, width), F32),
            pltpu.VMEM((cols + 2, rows, 9 * width), BF16),
            pltpu.VMEM((NY, NZ, chunk, channels), BF16),
            pltpu.VMEM((NY, NZ, chunk, channels), BF16),
            pltpu.VMEM((2, 2, chunk, channels), BF16),
            pltpu.VMEM((2, NZ, chunk, channels), BF16),
            pltpu.VMEM((2, half, channels), BF16),
            pltpu.VMEM((2, chunk, channels), BF16),
            pltpu.VMEM((4, block, 9 * width), F32),
            pltpu.VMEM((channels, NZ * chunk), BF16),
            pltpu.VMEM((4, block, 9 * width), BF16),
            pltpu.VMEM((2, block, 9 * width), BF16),
            pltpu.VMEM((block, 9 * width), BF16),
            pltpu.VMEM((block, 9 * width), BF16),
            pltpu.VMEM((2, cols, width), BF16),
            pltpu.SemaphoreType.DMA((MESSAGES,)),
            pltpu.SemaphoreType.DMA((MESSAGES,)),
            pltpu.SemaphoreType.DMA((10,)),
        ],
        compiler_params=pltpu.CompilerParams(
            collective_id=0, has_side_effects=True, vmem_limit_bytes=60 * 1024 * 1024
        ),
    )(x, upstream, weights.reshape(9, channels, width))
    input_grad = jnp.transpose(gi.reshape(own_cols, rows, channels), (1, 0, 2))
    return input_grad, gk.reshape(3, 3, block, width)


def solution(mesh):
    placed = (P("tile", "filt", "chan"), P("tile", None, "filt"), P(None, None, "chan", "filt"))
    return jax.shard_map(
        per_device,
        mesh=mesh,
        in_specs=placed,
        out_specs=(P("tile", "filt", "chan"), P(None, None, ("chan", "tile"), "filt")),
        check_vma=False,
    )
```

time: 211 us -> 79.5 us (0.38)
  the two profiles are of different devices: /device:TPU:1 before, /device:TPU:6 now
where the time goes in v1:
time: 79.5 us; the launch traced here: 79.4 us
  Pallas kernels  75.2 us (95%)
  local copies, waits for them, and re-layouts  3.53 us (4%)
    pallas_call x1, Pallas kernels, per_device(): pl.pallas_call(kernel, name='conv_backward', out_shape=(jax.ShapeDtypeStr...  75.2 us
    unnamed x2, local copies, waits for them, and re-layouts  3.53 us

profile of v1, /device:TPU:6, one launch (start us, length us, event | category | flops | bytes accessed | tf_op | source)
XLA Modules:
  0.0 79.4 jit_solution(8876831594728952984)
XLA Ops:
  0.6 75.2 %conv_backward.1 = (bf16[192,512]{1,0:T(8,128)(2,1)}, f32[9,128,128]{2,1,0:T(8,128)}) custom-call(bf16[192,512]{1,0:T(8,128)(2,1)} %bitcast.10, bf16[64,48,128]{2,1,0:T(8,128)(2,1)} %u_ref.1, bf16[9,512,128]{2,1,0:T(8,128)(2,1)} %bitcast.8), custom_call_target="tpu_custom_call" | custom-call | tf_op jit(solution)/shard_map/conv_backward/pallas_call | solution.py:308
  75.8 1.6 %copy.7 = bf16[64,3,512]{2,0,1:T(8,128)(2,1)} copy(bf16[64,3,512]{2,0,1:T(8,128)(2,1)} %bitcast.11) | data formatting | bytes 393216
  77.5 1.9 %copy.8 = f32[3,3,128,128]{3,2,1,0:T(8,128)} copy(f32[3,3,128,128]{3,2,1,0:T(8,128)} %bitcast.9) | data formatting | bytes 1179648

commit v2 on v0

v2 whole, which is shorter than its diff:
```python
from contextlib import nullcontext as mark

import jax
import jax.numpy as jnp
from jax import lax
from jax.experimental import pallas as pl
from jax.experimental.pallas import tpu as pltpu
from jax.sharding import PartitionSpec as P

BF16, F32 = jnp.bfloat16, jnp.float32
NY, NZ = 4, 4
UP, DOWN = 0, 1
BOTH = (UP, DOWN)
NEAR = (1, 3)
FAR_BLOCKS = ((2, 1), (3, 0))
Z_ROWS = 64


class Numbers:
    def __init__(self):
        self.known = {}

    def __call__(self, *key):
        return self.known.setdefault(key, len(self.known))


MESSAGES = 80


def kernel(
    x_ref, u_ref, k_ref, gi_ref, gk_ref,
    u_vm, kc, uf, s_buf, a_buf, p_buf, far_y, near_y, far_z, near_z, far2_y, near2_y, far2_z, near2_z,
    wacc, at, wb, wc_in, wz_out, wz_in, halo, ssem, rsem, lsem,
):
    rows, cols, width = u_ref.shape
    chunk = x_ref.shape[0]
    half = chunk // 2
    own_cols = chunk // rows
    group_cols = NZ * own_cols
    taps = 3 * width
    filt, tile = lax.axis_index("filt"), lax.axis_index("tile")
    y, z = lax.div(filt, NZ), lax.rem(filt, NZ)
    lo, core = lax.div(tile, 2), lax.rem(tile, 2)
    number = Numbers()

    def zed(step):
        return lax.rem(z + step, NZ)

    def ycoord(step):
        return lax.rem(y + step, NY)

    def at_y(direction):
        return {"filt": ycoord(NEAR[direction]) * NZ + z}

    def at_z(direction):
        return {"filt": y * NZ + zed(NEAR[direction])}

    def send(key, src, dst, peer):
        n = number(*key)
        return pltpu.make_async_remote_copy(
            src_ref=src, dst_ref=dst, send_sem=ssem.at[n], recv_sem=rsem.at[n],
            device_id=peer, device_id_type=pl.DeviceIdType.MESH,
        )

    started = []

    def start(copy):
        copy.start()
        started.append(copy)

    other_core = {"tile": lo * 2 + 1 - core}
    other_lo = {"tile": (1 - lo) * 2 + core}
    cross = {"tile": (1 - lo) * 2 + 1 - core}

    barrier = pltpu.get_barrier_semaphore()
    peers = [at_y(UP), at_y(DOWN), at_z(UP), at_z(DOWN), other_core, other_lo, cross]
    for peer in peers:
        pl.semaphore_signal(barrier, inc=1, device_id=peer, device_id_type=pl.DeviceIdType.MESH)

    upstream_copy = pltpu.make_async_copy(u_ref, u_vm, lsem.at[10])
    upstream_copy.start()
    own = pltpu.make_async_copy(x_ref, a_buf.at[0, z], lsem.at[9])
    own.start()
    weights = []
    for si in range(3):
        for ri in range(3):
            place = si * 3 + ri
            copy = pltpu.make_async_copy(
                k_ref.at[ri * 3 + si], kc.at[:, pl.ds(place * width, width)], lsem.at[place]
            )
            copy.start()
            weights.append(copy)
    with mark("a_barrier"):
        pl.semaphore_wait(barrier, len(peers))

    def part(h):
        return pl.ds(h * half, half)

    def z1(d, h):
        return send(("z1", d, h), x_ref.at[part(h)], a_buf.at[0, z, part(h)], at_z(d))

    def z2(d):
        slot = a_buf.at[0, zed(NEAR[1 - d]), part(d)]
        return send(("z2", d), slot, slot, at_z(d))

    def y1(d, b, h):
        src = x_ref.at[part(h)] if b == 0 else a_buf.at[0, zed(b), part(h)]
        return send(("y1", d, b, h), src, a_buf.at[NEAR[1 - d], zed(b), part(h)], at_y(d))

    def y2(d, b):
        return send(
            ("y2", d, b), a_buf.at[NEAR[1 - d], zed(b), part(d)], a_buf.at[2, zed(b), part(d)], at_y(d)
        )

    def wcore(k):
        return send(("wc", k), wb.at[2 * k + 1 - core], wc_in.at[k], other_core)

    def wlo():
        return send(("wz",), wz_out, wz_in, other_lo)

    def halo_down():
        return send(("halo", 0), u_ref.at[0], halo.at[1], {"tile": tile - 1})

    def halo_up():
        return send(("halo", 1), u_ref.at[rows - 1], halo.at[0], {"tile": tile + 1})

    class Reduce:
        def __init__(self, name, low, count, first, second, swap, bufs):
            self.name, self.low, self.count = name, low, count
            self.first, self.second, self.swap = first, second, swap
            self.far_in, self.near_in, self.far2_in, self.near2_in = bufs

        def block(self, i, j, h=None):
            low, count = self.low, self.count
            if h is not None:
                count //= 2
                low += h * count
            slot = (j, i) if self.swap else (i, j)
            return (*slot, pl.ds(low, count))

        def far(self, d, k):
            src = p_buf.at[self.block(2, FAR_BLOCKS[d][k])]
            return send((self.name, "far", d, k), src, self.far_in.at[d, k], self.first(d))

        def near(self, d, b):
            src = p_buf.at[self.block(NEAR[d], b)]
            return send((self.name, "near", d, b), src, self.near_in.at[d, b], self.first(d))

        def far2(self, d):
            src = p_buf.at[self.block(0, 2, d)]
            return send((self.name, "far2", d), src, self.far2_in.at[d], self.second(d))

        def near2(self, d):
            src = p_buf.at[self.block(0, NEAR[d])]
            return send((self.name, "near2", d), src, self.near2_in.at[d], self.second(d))

        def send_far(self, k):
            for d in BOTH:
                start(self.far(d, k))

        def send_near(self, b):
            d, k = {2: (UP, 0), 1: (UP, 1), 3: (DOWN, 0), 0: (DOWN, 1)}[b]
            start(self.near(1 - d, b))
            self.far(d, k).wait_recv()
            slot = self.block(NEAR[d], b)
            p_buf[slot] = (p_buf[slot].astype(F32) + self.far_in[d, k].astype(F32)).astype(BF16)
            start(self.near(d, b))

        def near_sum(self, b):
            for d in BOTH:
                self.near(d, b).wait_recv()
            own_term = p_buf[self.block(0, b)].astype(F32)
            return own_term + self.near_in[UP, b].astype(F32) + self.near_in[DOWN, b].astype(F32)

        def send_far2(self):
            p_buf[self.block(0, 2)] = self.near_sum(2).astype(BF16)
            for d in BOTH:
                start(self.far2(d))

        def send_near2(self, d):
            b, n = NEAR[d], self.count // 2
            total = self.near_sum(b)
            self.far2(d).wait_recv()
            p_buf[self.block(0, b, 1 - d)] = total[(1 - d) * n : (2 - d) * n].astype(BF16)
            p_buf[self.block(0, b, d)] = (
                total[d * n : (d + 1) * n] + self.far2_in[d].astype(F32)
            ).astype(BF16)
            start(self.near2(d))

        def finish(self):
            total = self.near_sum(0)
            for d in BOTH:
                self.near2(d).wait_recv()
            total += self.near2_in[UP].astype(F32) + self.near2_in[DOWN].astype(F32)
            place = pl.ds(self.low, self.count)
            gi_ref[place] = jnp.where(a_buf[0, z, place] > 0, total, 0.0).astype(BF16)

    red_z = Reduce("rz", 0, Z_ROWS, at_z, at_y, True, (far_z, near_z, far2_z, near2_z))
    red_y = Reduce("ry", Z_ROWS, chunk - Z_ROWS, at_y, at_z, False, (far_y, near_y, far2_y, near2_y))

    first, last = tile == 0, tile == 3

    @pl.when(jnp.logical_not(first))
    def _():
        halo_down().start()

    @pl.when(jnp.logical_not(last))
    def _():
        halo_up().start()

    for h in BOTH:
        for d in BOTH:
            start(z1(d, h ^ d))
            start(y1(d, 0, h ^ d))

    with mark("b_uf"):
        upstream_copy.wait()

        @pl.loop(0, rows)
        def _(i):
            uf[pl.ds(pl.multiple_of((i + 1) * cols, 8), cols), :] = u_vm[i].astype(F32)

    s_buf[1, :, 2 * taps :] = jnp.zeros((rows, taps), BF16)
    s_buf[cols, :, :taps] = jnp.zeros((rows, taps), BF16)
    bottom = (rows + 1) * cols
    with mark("c_halo"):

        @pl.when(first)
        def _():
            uf[:cols, :] = jnp.zeros((cols, width), F32)

        @pl.when(jnp.logical_not(first))
        def _():
            halo_up().wait_recv()
            uf[:cols, :] = halo[0].astype(F32)

        @pl.when(last)
        def _():
            uf[bottom:, :] = jnp.zeros((cols, width), F32)

        @pl.when(jnp.logical_not(last))
        def _():
            halo_down().wait_recv()
            uf[bottom:, :] = halo[1].astype(F32)

    with mark("d_im2col"):

        @pl.loop(0, cols)
        def _(j):
            for ri in range(3):
                value = uf[pl.ds((2 - ri) * cols + j, rows, stride=cols), :].astype(BF16)
                for si in range(3):
                    s_buf[j + si, :, pl.ds(si * taps + ri * width, width)] = value

        for copy in weights:
            copy.wait()

    def stacked(a):
        block = s_buf[pl.ds(ycoord(a) * group_cols + 1, group_cols)]
        return block.reshape(NZ * chunk, 3 * taps)

    def dgrad(a):
        with mark(f"dgrad{a}"):
            value = lax.dot_general(
                stacked(a), kc[...], (((1,), (1,)), ((), ())), preferred_element_type=F32
            ).astype(BF16)
            for place in range(NZ):
                p_buf[a, lax.rem(place - z + NZ, NZ)] = value[place * chunk : (place + 1) * chunk]

    def wgrad(a):
        with mark(f"wgrad{a}"):
            chunks = a_buf[a].reshape(NZ * chunk, a_buf.shape[3])
            at[...] = jnp.maximum(chunks, jnp.zeros((), BF16)).T
            value = jnp.dot(at[...], stacked(a), preferred_element_type=F32).reshape(wacc.shape)
            if a == 0:
                wacc[...] = value
            else:
                wacc[...] += value

    def pass_y(d, b):
        y1(d, b, d).wait_recv()
        start(y2(d, b))

    dgrad(2)
    with mark("01_z1_first"):
        for d in BOTH:
            z1(d, d).wait_recv()
            start(z2(d))
            for e in BOTH:
                start(y1(e, NEAR[1 - d], d))
        for d in BOTH:
            pass_y(d, 0)
    dgrad(1)
    dgrad(3)
    dgrad(0)
    with mark("02_z1_second"):
        for d in BOTH:
            z1(d, 1 - d).wait_recv()
            for e in BOTH:
                start(y1(e, NEAR[1 - d], 1 - d))
        for k in (0, 1):
            red_z.send_far(k)
    with mark("03_pass_first"):
        for d in BOTH:
            pass_y(d, NEAR[1 - d])
        for k in (0, 1):
            red_y.send_far(k)
    own.wait()
    with mark("04_z2"):
        for d in BOTH:
            z2(d).wait_recv()
            for e in BOTH:
                start(y1(e, 2, d))
    wgrad(0)
    with mark("05_pass_second"):
        for d in BOTH:
            pass_y(d, NEAR[d])
    with mark("06_rz_near"):
        for b in (2, 1, 3, 0):
            red_z.send_near(b)
    with mark("07_pass_far"):
        for d in BOTH:
            pass_y(d, 2)
    with mark("08_ry_near_21"):
        for b in (2, 1):
            red_y.send_near(b)
    with mark("09_rz_far2"):
        red_z.send_far2()
    with mark("10_y1_rest"):
        for b in range(NZ):
            for d in BOTH:
                y1(d, b, 1 - d).wait_recv()
    wgrad(3)
    wgrad(1)
    with mark("11_ry_near_30"):
        for b in (3, 0):
            red_y.send_near(b)
    with mark("12_rz_near2"):
        for d in BOTH:
            red_z.send_near2(d)
    with mark("13_y2"):
        for b in range(NZ):
            for d in BOTH:
                y2(d, b).wait_recv()
    wgrad(2)
    with mark("14_wcore"):
        wb[...] = wacc[...].astype(BF16)
        for k in (0, 1):
            start(wcore(k))
    with mark("15_ry_far2"):
        red_y.send_far2()
    with mark("16_wcore_in"):
        for k in (0, 1):
            wcore(k).wait_recv()
        wz_out[...] = (wacc[2 * (1 - lo) + core] + wc_in[1 - lo].astype(F32)).astype(BF16)
        start(wlo())
    with mark("17_ry_near2"):
        for d in BOTH:
            red_y.send_near2(d)
    with mark("18_rz_finish"):
        red_z.finish()
    with mark("19_ry_finish"):
        red_y.finish()
    with mark("20_wlo_in"):
        wlo().wait_recv()
        grad = wacc[tile] + wc_in[lo].astype(F32) + wz_in[...].astype(F32)
        for si in range(3):
            for ri in range(3):
                place = (si * 3 + ri) * width
                gk_ref[ri * 3 + si] = grad[:, place : place + width]
    with mark("21_sends"):
        for copy in started:
            copy.wait_send()

        @pl.when(jnp.logical_not(first))
        def _():
            halo_down().wait_send()

        @pl.when(jnp.logical_not(last))
        def _():
            halo_up().wait_send()


def write_out(gi_ref, gk_ref, gi_out, gk_out, sem):
    copies = [
        pltpu.make_async_copy(gi_ref, gi_out, sem.at[0]),
        pltpu.make_async_copy(gk_ref, gk_out, sem.at[1]),
    ]
    for copy in copies:
        copy.start()
    for copy in copies:
        copy.wait()


def per_device(saved_input, upstream, weights):
    rows, cols, width = upstream.shape
    own_cols, channels = saved_input.shape[1], saved_input.shape[2]
    chunk = own_cols * rows
    x = jnp.transpose(saved_input, (1, 0, 2)).reshape(chunk, channels)
    hbm = pl.BlockSpec(memory_space=pl.ANY)
    vmem = pl.BlockSpec(memory_space=pltpu.VMEM)
    block = channels // 4
    y_rows = chunk - Z_ROWS
    gi_shape, gk_shape = (chunk, channels), (9, block, width)

    def landing(n):
        return [
            pltpu.VMEM((2, 2, n, channels), BF16),
            pltpu.VMEM((2, NZ, n, channels), BF16),
        ]

    def landing2(n):
        return [pltpu.VMEM((2, n // 2, channels), BF16), pltpu.VMEM((2, n, channels), BF16)]

    gi, gk = pl.pallas_call(
        kernel,
        name="conv_backward",
        out_shape=(pltpu.VMEM(gi_shape, BF16), pltpu.VMEM(gk_shape, F32)),
        in_specs=[hbm, hbm, hbm],
        out_specs=(vmem, vmem),
        scratch_shapes=[
            pltpu.VMEM((rows, cols, width), BF16),
            pltpu.VMEM((channels, 9 * width), BF16),
            pltpu.VMEM(((rows + 2) * cols, width), F32),
            pltpu.VMEM((cols + 2, rows, 9 * width), BF16),
            pltpu.VMEM((NY, NZ, chunk, channels), BF16),
            pltpu.VMEM((NY, NZ, chunk, channels), BF16),
            *landing(y_rows),
            *landing(Z_ROWS),
            *landing2(y_rows),
            *landing2(Z_ROWS),
            pltpu.VMEM((4, block, 9 * width), F32),
            pltpu.VMEM((channels, NZ * chunk), BF16),
            pltpu.VMEM((4, block, 9 * width), BF16),
            pltpu.VMEM((2, block, 9 * width), BF16),
            pltpu.VMEM((block, 9 * width), BF16),
            pltpu.VMEM((block, 9 * width), BF16),
            pltpu.VMEM((2, cols, width), BF16),
            pltpu.SemaphoreType.DMA((MESSAGES,)),
            pltpu.SemaphoreType.DMA((MESSAGES,)),
            pltpu.SemaphoreType.DMA((11,)),
        ],
        compiler_params=pltpu.CompilerParams(
            collective_id=0, has_side_effects=True, vmem_limit_bytes=56 * 1024 * 1024
        ),
    )(x, upstream, weights.reshape(9, channels, width))
    gi, gk = pl.pallas_call(
        write_out,
        name="write_out",
        out_shape=(jax.ShapeDtypeStruct(gi_shape, BF16), jax.ShapeDtypeStruct(gk_shape, F32)),
        in_specs=[vmem, vmem],
        out_specs=(hbm, hbm),
        scratch_shapes=[pltpu.SemaphoreType.DMA((2,))],
        compiler_params=pltpu.CompilerParams(vmem_limit_bytes=1024 * 1024),
    )(gi, gk)
    input_grad = jnp.transpose(gi.reshape(own_cols, rows, channels), (1, 0, 2))
    return input_grad, gk.reshape(3, 3, block, width)


def solution(mesh):
    placed = (P("tile", "filt", "chan"), P("tile", None, "filt"), P(None, None, "chan", "filt"))
    return jax.shard_map(
        per_device,
        mesh=mesh,
        in_specs=placed,
        out_specs=(P("tile", "filt", "chan"), P(None, None, ("chan", "tile"), "filt")),
        check_vma=False,
    )
```

time: 211 us -> 74 us (0.35)
  waiting for transfers between devices: 88.8 us -> 0 us
  Pallas kernels: 0 us -> 73.3 us
  local copies, waits for them, and re-layouts: 67.5 us -> 0 us
  matrix products: 18.5 us -> 0 us
  between operations: 14 us -> 0.64 us
  starting transfers between devices: 11.5 us -> 0 us
  other arithmetic: 9.42 us -> 0 us
    pallas_call x0 -> x2, Pallas kernels: none -> 73.3 us  [the longest x1 72.4 us: per_device(): pl.pallas_call(kernel, name='conv_backward', out_shape=(pltpu.VMEM(gi_sha...]
    all_gather x1 -> x0, waiting for transfers between devices: 50.9 us -> none  [per_device(): gathered = lax.all_gather(active, 'filt', axis=1, tiled=True)]
    dot_general x1 -> x0, local copies, waits for them, and re-layouts: 36.7 us -> none  [per_device(): jnp.dot(stacked_input.T, upstream.reshape(height * breadth, out_width), p...]
    reduce_scatter x2 -> x0, waiting for transfers between devices: 33.6 us -> none  [the longest x1 23.7 us: per_device(): lax.psum_scatter(kernel_part.astype(jnp.bfloat16), 'tile', scatter_dimens...]
    unnamed x18 -> x0, local copies, waits for them, and re-layouts: 19.6 us -> none
    dot_general x2 -> x0, matrix products: 18.5 us -> none  [the longest x1 14 us: per_device(): jnp.dot(stacked_input.T, upstream.reshape(height * breadth, out_width), p...]
    ppermute x4 -> x0, starting transfers between devices: 11.3 us -> none  [the longest x2 6.83 us: padded_2(): before = lax.ppermute(last, axis, up)]
    ppermute x4 -> x0, waiting for transfers between devices: 4.29 us -> none  [the longest x2 4.29 us: padded_2(): after = lax.ppermute(leading, axis, down)]
  transfers between devices with their start and end apart: 7 -> 0, of which waited for: 5 -> 0; matrix products, arithmetic and copies ran while one was open for 39% -> 0% of each run, Pallas kernels for 0% -> 0%
where the time goes in v2:
time: 74 us; the launch traced here: 73.9 us
  Pallas kernels  73.3 us (99%)
    pallas_call x1, Pallas kernels, per_device(): pl.pallas_call(kernel, name='conv_backward', out_shape=(pltpu.VMEM(gi_sha...  72.4 us

profile of v2, /device:TPU:1, one launch (start us, length us, event | category | flops | bytes accessed | tf_op | source)
XLA Modules:
  0.0 73.9 jit_solution(17322707206136013480)
XLA Ops:
  0.6 72.4 %conv_backward.1 = (bf16[192,512]{1,0:T(8,128)(2,1)S(1)}, f32[9,128,128]{2,1,0:T(8,128)S(1)}) custom-call(bf16[192,512]{1,0:T(8,128)(2,1)} %bitcast.9, bf16[64,48,128]{2,1,0:T(8,128)(2,1)} %u_ref.1, bf16[9,512,128]{2,1,0:T(8,128)(2,1)} %bitcast.8), custom_call_target="tpu_custom_call" | custom-call | tf_op jit(solution)/shard_map/conv_backward/pallas_call | solution.py:415
  73.0 0.9 %write_out.1 = (bf16[192,512]{1,0:T(8,128)(2,1)}, f32[9,128,128]{2,1,0:T(8,128)}) custom-call(bf16[192,512]{1,0:T(8,128)(2,1)S(1)} %get-tuple-element.6.gi_ref, f32[9,128,128]{2,1,0:T(8,128)S(1)} %get-tuple-element.7.gk_ref), custom_call_target="tpu_custom_call" | custom-call | tf_op jit(solution)/shard_map/write_out/pallas_call | solution.py:447

commit v3 on v2

--- a/solution.py
+++ b/solution.py
@@ -1,3 +1,4 @@
+import functools
 from contextlib import nullcontext as mark
 
 import jax
@@ -13,7 +14,8 @@
 BOTH = (UP, DOWN)
 NEAR = (1, 3)
 FAR_BLOCKS = ((2, 1), (3, 0))
-Z_ROWS = 64
+RELAY = {2: (UP, 0), 1: (UP, 1), 3: (DOWN, 0), 0: (DOWN, 1)}
+Z_ROWS = 96
 
 
 class Numbers:
@@ -24,7 +26,20 @@
         return self.known.setdefault(key, len(self.known))
 
 
-MESSAGES = 80
+MESSAGES = 67
+
+ORDER = (
+    "pass00", "dgrad2", "ry_far10", "z1a1", "z1a0", "dgrad1",
+    "ry_far01", "dgrad0", "dgrad3", "rz_dir0", "rz_far01", "ry_dir2",
+    "rz_dir1", "rz_far11", "ry_far00", "z2_1", "z1b0", "ry_dir1",
+    "pass11", "z2_0", "rz_far00", "rz_far10", "pass03", "ry_dep3",
+    "z1b1", "ry_dep2", "pass12", "ry_dir3", "pass13", "rz_dir2",
+    "rz_dep2", "wgrad0", "pass02", "ry_dep1", "rz_dep0", "rz_dir3",
+    "pass01", "pass10", "ry_far2", "wgrad1", "rz_dep3", "rz_dep1",
+    "rz_far2", "wgrad3", "ry_near21", "ry_near20", "ry_far11", "wgrad2",
+    "wcore", "rz_near20", "wlo", "rz_near21", "ry_dir0", "ry_dep0",
+    "ry_fin", "rz_fin", "wfin",
+)
 
 
 def kernel(
@@ -154,13 +169,14 @@
             src = p_buf.at[self.block(0, NEAR[d])]
             return send((self.name, "near2", d), src, self.near2_in.at[d], self.second(d))
 
-        def send_far(self, k):
-            for d in BOTH:
-                start(self.far(d, k))
-
-        def send_near(self, b):
-            d, k = {2: (UP, 0), 1: (UP, 1), 3: (DOWN, 0), 0: (DOWN, 1)}[b]
-            start(self.near(1 - d, b))
+        def send_far(self, d, k):
+            start(self.far(d, k))
+
+        def send_direct(self, b):
+            start(self.near(1 - RELAY[b][0], b))
+
+        def send_relayed(self, b):
+            d, k = RELAY[b]
             self.far(d, k).wait_recv()
             slot = self.block(NEAR[d], b)
             p_buf[slot] = (p_buf[slot].astype(F32) + self.far_in[d, k].astype(F32)).astype(BF16)
@@ -260,114 +276,101 @@
         return block.reshape(NZ * chunk, 3 * taps)
 
     def dgrad(a):
-        with mark(f"dgrad{a}"):
-            value = lax.dot_general(
-                stacked(a), kc[...], (((1,), (1,)), ((), ())), preferred_element_type=F32
-            ).astype(BF16)
-            for place in range(NZ):
-                p_buf[a, lax.rem(place - z + NZ, NZ)] = value[place * chunk : (place + 1) * chunk]
+        value = lax.dot_general(
+            stacked(a), kc[...], (((1,), (1,)), ((), ())), preferred_element_type=F32
+        ).astype(BF16)
+        for place in range(NZ):
+            p_buf[a, lax.rem(place - z + NZ, NZ)] = value[place * chunk : (place + 1) * chunk]
 
     def wgrad(a):
-        with mark(f"wgrad{a}"):
-            chunks = a_buf[a].reshape(NZ * chunk, a_buf.shape[3])
-            at[...] = jnp.maximum(chunks, jnp.zeros((), BF16)).T
-            value = jnp.dot(at[...], stacked(a), preferred_element_type=F32).reshape(wacc.shape)
-            if a == 0:
-                wacc[...] = value
-            else:
-                wacc[...] += value
+        chunks = a_buf[a].reshape(NZ * chunk, a_buf.shape[3])
+        at[...] = jnp.maximum(chunks, jnp.zeros((), BF16)).T
+        value = jnp.dot(at[...], stacked(a), preferred_element_type=F32).reshape(wacc.shape)
+        if a == 0:
+            wacc[...] = value
+        else:
+            wacc[...] += value
+
+    def z1_first(d):
+        z1(d, d).wait_recv()
+        start(z2(d))
+        for e in BOTH:
+            start(y1(e, NEAR[1 - d], d))
+
+    def z1_second(d):
+        z1(d, 1 - d).wait_recv()
+        for e in BOTH:
+            start(y1(e, NEAR[1 - d], 1 - d))
+
+    def z2_in(d):
+        z2(d).wait_recv()
+        for e in BOTH:
+            start(y1(e, 2, d))
 
     def pass_y(d, b):
         y1(d, b, d).wait_recv()
         start(y2(d, b))
 
-    dgrad(2)
-    with mark("01_z1_first"):
-        for d in BOTH:
-            z1(d, d).wait_recv()
-            start(z2(d))
-            for e in BOTH:
-                start(y1(e, NEAR[1 - d], d))
-        for d in BOTH:
-            pass_y(d, 0)
-    dgrad(1)
-    dgrad(3)
-    dgrad(0)
-    with mark("02_z1_second"):
-        for d in BOTH:
-            z1(d, 1 - d).wait_recv()
-            for e in BOTH:
-                start(y1(e, NEAR[1 - d], 1 - d))
-        for k in (0, 1):
-            red_z.send_far(k)
-    with mark("03_pass_first"):
-        for d in BOTH:
-            pass_y(d, NEAR[1 - d])
-        for k in (0, 1):
-            red_y.send_far(k)
-    own.wait()
-    with mark("04_z2"):
-        for d in BOTH:
-            z2(d).wait_recv()
-            for e in BOTH:
-                start(y1(e, 2, d))
-    wgrad(0)
-    with mark("05_pass_second"):
-        for d in BOTH:
-            pass_y(d, NEAR[d])
-    with mark("06_rz_near"):
-        for b in (2, 1, 3, 0):
-            red_z.send_near(b)
-    with mark("07_pass_far"):
-        for d in BOTH:
-            pass_y(d, 2)
-    with mark("08_ry_near_21"):
-        for b in (2, 1):
-            red_y.send_near(b)
-    with mark("09_rz_far2"):
-        red_z.send_far2()
-    with mark("10_y1_rest"):
+    def rest_y(d):
         for b in range(NZ):
-            for d in BOTH:
-                y1(d, b, 1 - d).wait_recv()
-    wgrad(3)
-    wgrad(1)
-    with mark("11_ry_near_30"):
-        for b in (3, 0):
-            red_y.send_near(b)
-    with mark("12_rz_near2"):
-        for d in BOTH:
-            red_z.send_near2(d)
-    with mark("13_y2"):
+            y1(d, b, 1 - d).wait_recv()
+
+    def all_y2():
         for b in range(NZ):
             for d in BOTH:
                 y2(d, b).wait_recv()
-    wgrad(2)
-    with mark("14_wcore"):
+
+    def wcore_out():
         wb[...] = wacc[...].astype(BF16)
         for k in (0, 1):
             start(wcore(k))
-    with mark("15_ry_far2"):
-        red_y.send_far2()
-    with mark("16_wcore_in"):
+
+    def wlo_out():
         for k in (0, 1):
             wcore(k).wait_recv()
         wz_out[...] = (wacc[2 * (1 - lo) + core] + wc_in[1 - lo].astype(F32)).astype(BF16)
         start(wlo())
-    with mark("17_ry_near2"):
-        for d in BOTH:
-            red_y.send_near2(d)
-    with mark("18_rz_finish"):
-        red_z.finish()
-    with mark("19_ry_finish"):
-        red_y.finish()
-    with mark("20_wlo_in"):
+
+    def wgrad_out():
         wlo().wait_recv()
         grad = wacc[tile] + wc_in[lo].astype(F32) + wz_in[...].astype(F32)
         for si in range(3):
             for ri in range(3):
                 place = (si * 3 + ri) * width
                 gk_ref[ri * 3 + si] = grad[:, place : place + width]
+
+    steps = {
+        "wcore": wcore_out,
+        "wlo": wlo_out,
+        "wfin": wgrad_out,
+        "wgrad0": lambda: (own.wait(), wgrad(0)),
+        "wgrad3": lambda: (rest_y(UP), wgrad(3)),
+        "wgrad1": lambda: (rest_y(DOWN), wgrad(1)),
+        "wgrad2": lambda: (all_y2(), wgrad(2)),
+    }
+    for a in range(NY):
+        steps[f"dgrad{a}"] = functools.partial(dgrad, a)
+    for d in BOTH:
+        steps[f"z1a{d}"] = functools.partial(z1_first, d)
+        steps[f"z1b{d}"] = functools.partial(z1_second, d)
+        steps[f"z2_{d}"] = functools.partial(z2_in, d)
+        for b in range(NZ):
+            steps[f"pass{d}{b}"] = functools.partial(pass_y, d, b)
+    for red in (red_y, red_z):
+        for d in BOTH:
+            for k in (0, 1):
+                steps[f"{red.name}_far{k}{d}"] = functools.partial(red.send_far, d, k)
+            steps[f"{red.name}_near2{d}"] = functools.partial(red.send_near2, d)
+        for b in range(NZ):
+            steps[f"{red.name}_dir{b}"] = functools.partial(red.send_direct, b)
+            steps[f"{red.name}_dep{b}"] = functools.partial(red.send_relayed, b)
+        steps[f"{red.name}_far2"] = red.send_far2
+        steps[f"{red.name}_fin"] = red.finish
+    assert set(ORDER) == set(steps) and len(ORDER) == len(steps)
+    for n, name in enumerate(ORDER):
+        with mark(f"{n:02}_{name}"):
+            steps[name]()
+    assert len(number.known) <= MESSAGES
     with mark("21_sends"):
         for copy in started:
             copy.wait_send()

time: 74 us -> 63.1 us (0.85)
  Pallas kernels: 73.3 us -> 62.3 us
    pallas_call x1, Pallas kernels: 72.4 us -> 61.4 us  [per_device(): pl.pallas_call(kernel, name='conv_backward', out_shape=(pltpu.VMEM(gi_sha...]
where the time goes in v3:
time: 63.1 us; the launch traced here: 63 us
  Pallas kernels  62.3 us (99%)
  between operations  0.64 us (1%)
    pallas_call x1, Pallas kernels, per_device(): pl.pallas_call(kernel, name='conv_backward', out_shape=(pltpu.VMEM(gi_sha...  61.4 us

profile of v3, /device:TPU:1, one launch (start us, length us, event | category | flops | bytes accessed | tf_op | source)
XLA Modules:
  0.0 63.0 jit_solution(7824514091024462451)
XLA Ops:
  0.6 61.4 %conv_backward.1 = (bf16[192,512]{1,0:T(8,128)(2,1)S(1)}, f32[9,128,128]{2,1,0:T(8,128)S(1)}) custom-call(bf16[192,512]{1,0:T(8,128)(2,1)} %bitcast.9, bf16[64,48,128]{2,1,0:T(8,128)(2,1)} %u_ref.1, bf16[9,512,128]{2,1,0:T(8,128)(2,1)} %bitcast.8), custom_call_target="tpu_custom_call" | custom-call | tf_op jit(solution)/shard_map/conv_backward/pallas_call | solution.py:418
  62.1 0.9 %write_out.1 = (bf16[192,512]{1,0:T(8,128)(2,1)}, f32[9,128,128]{2,1,0:T(8,128)}) custom-call(bf16[192,512]{1,0:T(8,128)(2,1)S(1)} %get-tuple-element.6.gi_ref, f32[9,128,128]{2,1,0:T(8,128)S(1)} %get-tuple-element.7.gk_ref), custom_call_target="tpu_custom_call" | custom-call | tf_op jit(solution)/shard_map/write_out/pallas_call | solution.py:450

commit v4 on v3

v4 whole, which is shorter than its diff:
```python
import functools
import math
from contextlib import nullcontext as mark

import jax
import jax.numpy as jnp
from jax import lax
from jax.experimental import pallas as pl
from jax.experimental.pallas import tpu as pltpu
from jax.sharding import PartitionSpec as P

BF16, F32 = jnp.bfloat16, jnp.float32
NY, NZ = 4, 4
UP, DOWN = 0, 1
BOTH = (UP, DOWN)
NEAR = (1, 3)
FAR_BLOCKS = ((2, 1), (3, 0))
RELAY = {2: (UP, 0), 1: (UP, 1), 3: (DOWN, 0), 0: (DOWN, 1)}
CLASSES = (("rz", "z", 64), ("ry", "y", 64), ("rw", "y", 64))
W_PARTS = 3
MESSAGES = 89

ORDER = (
    "pass00", "pass10", "dgrad2", "ry_far00", "z2_1", "z2_0", "rw_far00",
    "y1_011", "y1_130", "y1_030", "dgrad1", "y1_111", "dgrad0", "y1_031",
    "y1_110", "y1_010", "dgrad3", "ry_far01", "rz_far01", "y1_131", "y1_121",
    "rz_far00", "y1_020", "y1_120", "y1_021", "rz_far10", "rz_dir3", "pass03",
    "pass11", "rz_dir2", "rz_dir0", "rz_far11", "pass12", "pass01", "pass13",
    "pass02", "rz_dep2", "ry_dir2", "rz_dep3", "rz_dep0", "ry_dep2", "rw_dep2",
    "rz_dep1", "rz_dir1", "rw_far10", "rw_dir2", "rw_far01", "ry_far10", "wgrad0",
    "wgrad1", "wgrad3", "rw_dir1", "wgrad2_0", "wcore_0", "ry_far2", "ry_dir3",
    "rw_far11", "wgrad2_1", "ry_dep3", "ry_far11", "rw_far2", "wcore_1", "wlo_0",
    "rw_dep1", "wgrad2_2", "ry_dir1", "rw_dep3", "ry_dep1", "rw_dir3", "wlo_1",
    "ry_near21", "rz_far2", "rw_near20", "wfin_0", "rw_dir0", "ry_near20", "wcore_2",
    "rw_near21", "rz_near20", "rz_near21", "ry_dep0", "wlo_2", "ry_dir0", "rw_dep0",
    "rz_fin", "ry_fin", "wfin_1", "rw_fin", "wfin_2",
)


class Message:
    def __init__(self, make, key, landed):
        self.make, self.key, self.landed = make, key, landed

    def arrive(self):
        if self.key not in self.landed:
            self.landed.add(self.key)
            self.make().wait_recv()


def kernel(
    x_ref, u_ref, k_ref, gi_ref, gk_ref,
    u_vm, kc, uf, s_buf, a_buf, p_buf, wacc, at, wb, wc_in, wz_out, wz_in, halo, ssem, rsem, lsem, *landing,
):
    rows, cols, width = u_ref.shape
    chunk = x_ref.shape[0]
    half = chunk // 2
    own_cols = chunk // rows
    group_cols = NZ * own_cols
    taps = 3 * width
    filt, tile = lax.axis_index("filt"), lax.axis_index("tile")
    y, z = lax.div(filt, NZ), lax.rem(filt, NZ)
    lo, core = lax.div(tile, 2), lax.rem(tile, 2)
    numbers, landed, sent = {}, set(), []

    def zed(step):
        return lax.rem(z + step, NZ)

    def ycoord(step):
        return lax.rem(y + step, NY)

    def at_y(direction):
        return {"filt": ycoord(NEAR[direction]) * NZ + z}

    def at_z(direction):
        return {"filt": y * NZ + zed(NEAR[direction])}

    def message(key, src, dst, peer, send_sem=None):
        n = numbers.setdefault(key, len(numbers))

        def make():
            return pltpu.make_async_remote_copy(
                src_ref=src, dst_ref=dst, send_sem=ssem.at[0] if send_sem is None else send_sem,
                recv_sem=rsem.at[n], device_id=peer, device_id_type=pl.DeviceIdType.MESH,
            )

        return Message(make, key, landed)

    def start(move):
        copy = move.make()
        copy.start()
        sent.append(math.prod(copy.src_ref.shape) * 2)

    def arrive(move):
        move.arrive()

    other_core = {"tile": lo * 2 + 1 - core}
    other_lo = {"tile": (1 - lo) * 2 + core}
    cross = {"tile": (1 - lo) * 2 + 1 - core}

    barrier = pltpu.get_barrier_semaphore()
    peers = [at_y(UP), at_y(DOWN), at_z(UP), at_z(DOWN), other_core, other_lo, cross]
    for peer in peers:
        pl.semaphore_signal(barrier, inc=1, device_id=peer, device_id_type=pl.DeviceIdType.MESH)

    upstream_copy = pltpu.make_async_copy(u_ref, u_vm, lsem.at[10])
    upstream_copy.start()
    own = pltpu.make_async_copy(x_ref, a_buf.at[0, z], lsem.at[9])
    own.start()
    weights = []
    for si in range(3):
        for ri in range(3):
            place = si * 3 + ri
            copy = pltpu.make_async_copy(
                k_ref.at[ri * 3 + si], kc.at[:, pl.ds(place * width, width)], lsem.at[place]
            )
            copy.start()
            weights.append(copy)
    with mark("a_barrier"):
        pl.semaphore_wait(barrier, len(peers))

    def part(h):
        return pl.ds(h * half, half)

    def z1(d, h):
        return message(("z1", d, h), x_ref.at[part(h)], a_buf.at[0, z, part(h)], at_z(d))

    def z2(d):
        slot = a_buf.at[0, zed(NEAR[1 - d]), part(d)]
        return message(("z2", d), slot, slot, at_z(d))

    def y1(d, b, h):
        src = x_ref.at[part(h)] if b == 0 else a_buf.at[0, zed(b), part(h)]
        return message(("y1", d, b, h), src, a_buf.at[NEAR[1 - d], zed(b), part(h)], at_y(d))

    def y2(d, b):
        return message(
            ("y2", d, b), a_buf.at[NEAR[1 - d], zed(b), part(d)], a_buf.at[2, zed(b), part(d)], at_y(d)
        )

    def columns(p):
        return pl.ds(p * taps, taps)

    def wcore(k, p):
        src = wb.at[2 * k + 1 - core, :, columns(p)]
        return message(("wc", k, p), src, wc_in.at[k, :, columns(p)], other_core)

    def wlo(p):
        return message(("wz", p), wz_out.at[:, columns(p)], wz_in.at[:, columns(p)], other_lo)

    def halo_down():
        return message(("halo", 0), u_ref.at[0], halo.at[1], {"tile": tile - 1}, lsem.at[11]).make()

    def halo_up():
        return message(("halo", 1), u_ref.at[rows - 1], halo.at[0], {"tile": tile + 1}, lsem.at[12]).make()

    class Reduce:
        def __init__(self, name, ring, low, count, bufs):
            self.name, self.low, self.count = name, low, count
            self.swap = ring == "z"
            self.first, self.second = (at_z, at_y) if self.swap else (at_y, at_z)
            self.far_in, self.near_in, self.far2_in, self.near2_in = bufs

        def block(self, i, j, h=None):
            low, count = self.low, self.count
            if h is not None:
                count //= 2
                low += h * count
            slot = (j, i) if self.swap else (i, j)
            return (*slot, pl.ds(low, count))

        def far(self, d, k):
            src = p_buf.at[self.block(2, FAR_BLOCKS[d][k])]
            return message((self.name, "far", d, k), src, self.far_in.at[d, k], self.first(d))

        def near(self, d, b):
            src = p_buf.at[self.block(NEAR[d], b)]
            return message((self.name, "near", d, b), src, self.near_in.at[d, b], self.first(d))

        def far2(self, d):
            src = p_buf.at[self.block(0, 2, d)]
            return message((self.name, "far2", d), src, self.far2_in.at[d], self.second(d))

        def near2(self, d):
            src = p_buf.at[self.block(0, NEAR[d])]
            return message((self.name, "near2", d), src, self.near2_in.at[d], self.second(d))

        def send_far(self, d, k):
            start(self.far(d, k))

        def send_direct(self, b):
            start(self.near(1 - RELAY[b][0], b))

        def send_relayed(self, b):
            d, k = RELAY[b]
            arrive(self.far(d, k))
            slot = self.block(NEAR[d], b)
            p_buf[slot] = (p_buf[slot].astype(F32) + self.far_in[d, k].astype(F32)).astype(BF16)
            start(self.near(d, b))

        def near_sum(self, b):
            for d in BOTH:
                arrive(self.near(d, b))
            own_term = p_buf[self.block(0, b)].astype(F32)
            return own_term + self.near_in[UP, b].astype(F32) + self.near_in[DOWN, b].astype(F32)

        def send_far2(self):
            p_buf[self.block(0, 2)] = self.near_sum(2).astype(BF16)
            for d in BOTH:
                start(self.far2(d))

        def send_near2(self, d):
            b, n = NEAR[d], self.count // 2
            total = self.near_sum(b)
            arrive(self.far2(d))
            p_buf[self.block(0, b, 1 - d)] = total[(1 - d) * n : (2 - d) * n].astype(BF16)
            p_buf[self.block(0, b, d)] = (
                total[d * n : (d + 1) * n] + self.far2_in[d].astype(F32)
            ).astype(BF16)
            start(self.near2(d))

        def finish(self):
            total = self.near_sum(0)
            for d in BOTH:
                arrive(self.near2(d))
            total += self.near2_in[UP].astype(F32) + self.near2_in[DOWN].astype(F32)
            place = pl.ds(self.low, self.count)
            gi_ref[place] = jnp.where(a_buf[0, z, place] > 0, total, 0.0).astype(BF16)

    first, last = tile == 0, tile == 3

    @pl.when(jnp.logical_not(first))
    def _():
        halo_down().start()

    @pl.when(jnp.logical_not(last))
    def _():
        halo_up().start()

    for h in BOTH:
        for d in BOTH:
            start(z1(d, h ^ d))
            start(y1(d, 0, h ^ d))

    with mark("b_uf"):
        upstream_copy.wait()

        @pl.loop(0, rows)
        def _(i):
            uf[pl.ds(pl.multiple_of((i + 1) * cols, 8), cols), :] = u_vm[i].astype(F32)

    s_buf[1, :, 2 * taps :] = jnp.zeros((rows, taps), BF16)
    s_buf[cols, :, :taps] = jnp.zeros((rows, taps), BF16)
    bottom = (rows + 1) * cols
    with mark("c_halo"):

        @pl.when(first)
        def _():
            uf[:cols, :] = jnp.zeros((cols, width), F32)

        @pl.when(jnp.logical_not(first))
        def _():
            halo_up().wait_recv()
            uf[:cols, :] = halo[0].astype(F32)

        @pl.when(last)
        def _():
            uf[bottom:, :] = jnp.zeros((cols, width), F32)

        @pl.when(jnp.logical_not(last))
        def _():
            halo_down().wait_recv()
            uf[bottom:, :] = halo[1].astype(F32)

    with mark("d_im2col"):

        @pl.loop(0, cols)
        def _(j):
            for ri in range(3):
                value = uf[pl.ds((2 - ri) * cols + j, rows, stride=cols), :].astype(BF16)
                for si in range(3):
                    s_buf[j + si, :, pl.ds(si * taps + ri * width, width)] = value

        for copy in weights:
            copy.wait()

    def stacked(a, lanes=slice(None)):
        block = s_buf[pl.ds(ycoord(a) * group_cols + 1, group_cols), :, lanes]
        return block.reshape(NZ * chunk, block.shape[2])

    def dgrad(a):
        value = lax.dot_general(
            stacked(a), kc[...], (((1,), (1,)), ((), ())), preferred_element_type=F32
        ).astype(BF16)
        for place in range(NZ):
            p_buf[a, lax.rem(place - z + NZ, NZ)] = value[place * chunk : (place + 1) * chunk]

    def activate(a):
        chunks = a_buf[a].reshape(NZ * chunk, a_buf.shape[3])
        at[...] = jnp.maximum(chunks, jnp.zeros((), BF16)).T

    def wgrad(a):
        activate(a)
        value = jnp.dot(at[...], stacked(a), preferred_element_type=F32).reshape(wacc.shape)
        if a == 0:
            wacc[...] = value
        else:
            wacc[...] += value

    def wgrad_z():
        own.wait()
        for d in BOTH:
            for h in BOTH:
                arrive(z1(d, h))
            arrive(z2(d))
        wgrad(0)

    def wgrad_y(d):
        for b in range(NZ):
            for h in BOTH:
                arrive(y1(d, b, h))
        wgrad(NEAR[1 - d])

    def wgrad_last(p):
        if p == 0:
            for b in range(NZ):
                for d in BOTH:
                    arrive(y2(d, b))
            activate(2)
        value = jnp.dot(at[...], stacked(2, columns(p)), preferred_element_type=F32)
        wacc[:, :, columns(p)] += value.reshape(wacc.shape[0], wacc.shape[1], taps)

    def wcore_out(p):
        wb[:, :, columns(p)] = wacc[:, :, columns(p)].astype(BF16)
        for k in (0, 1):
            start(wcore(k, p))

    def wlo_out(p):
        for k in (0, 1):
            arrive(wcore(k, p))
        total = wacc[2 * (1 - lo) + core, :, columns(p)] + wc_in[1 - lo, :, columns(p)].astype(F32)
        wz_out[:, columns(p)] = total.astype(BF16)
        start(wlo(p))

    def wgrad_out(p):
        arrive(wlo(p))
        grad = wacc[tile, :, columns(p)] + wc_in[lo, :, columns(p)].astype(F32)
        grad += wz_in[:, columns(p)].astype(F32)
        for ri in range(3):
            gk_ref[ri * 3 + p] = grad[:, ri * width : (ri + 1) * width]

    def pass_z(d):
        arrive(z1(d, d))
        start(z2(d))

    def pass_to_y(e, b, h):
        arrive(z2(h) if b == 2 else z1(UP if b == 3 else DOWN, h))
        start(y1(e, b, h))

    def pass_y(d, b):
        arrive(y1(d, b, d))
        start(y2(d, b))

    steps = {
        "wgrad0": wgrad_z,
        "wgrad3": functools.partial(wgrad_y, UP),
        "wgrad1": functools.partial(wgrad_y, DOWN),
    }
    for a in range(NY):
        steps[f"dgrad{a}"] = functools.partial(dgrad, a)
    for d in BOTH:
        steps[f"z2_{d}"] = functools.partial(pass_z, d)
        for b in range(NZ):
            steps[f"pass{d}{b}"] = functools.partial(pass_y, d, b)
        for b in (1, 2, 3):
            for h in BOTH:
                steps[f"y1_{d}{b}{h}"] = functools.partial(pass_to_y, d, b, h)
    for p in range(W_PARTS):
        steps[f"wgrad2_{p}"] = functools.partial(wgrad_last, p)
        steps[f"wcore_{p}"] = functools.partial(wcore_out, p)
        steps[f"wlo_{p}"] = functools.partial(wlo_out, p)
        steps[f"wfin_{p}"] = functools.partial(wgrad_out, p)
    low = 0
    for n, (name, ring, count) in enumerate(CLASSES):
        red = Reduce(name, ring, low, count, landing[4 * n : 4 * n + 4])
        low += count
        for d in BOTH:
            for k in (0, 1):
                steps[f"{name}_far{k}{d}"] = functools.partial(red.send_far, d, k)
            steps[f"{name}_near2{d}"] = functools.partial(red.send_near2, d)
        for b in range(NZ):
            steps[f"{name}_dir{b}"] = functools.partial(red.send_direct, b)
            steps[f"{name}_dep{b}"] = functools.partial(red.send_relayed, b)
        steps[f"{name}_far2"] = red.send_far2
        steps[f"{name}_fin"] = red.finish
    assert set(ORDER) == set(steps) and len(ORDER) == len(steps)
    for n, name in enumerate(ORDER):
        with mark(f"{n:03}_{name}"):
            steps[name]()
    assert len(numbers) == MESSAGES
    with mark("y_sends"):
        column = rows * 9 * width * 2
        assert sum(sent) % column == 0
        everything = s_buf.at[pl.ds(0, sum(sent) // column)]
        pltpu.make_async_copy(everything, everything, ssem.at[0]).wait()

        @pl.when(jnp.logical_not(first))
        def _():
            halo_down().wait_send()

        @pl.when(jnp.logical_not(last))
        def _():
            halo_up().wait_send()


def write_out(gi_ref, gk_ref, gi_out, gk_out, sem):
    copies = [
        pltpu.make_async_copy(gi_ref, gi_out, sem.at[0]),
        pltpu.make_async_copy(gk_ref, gk_out, sem.at[1]),
    ]
    for copy in copies:
        copy.start()
    for copy in copies:
        copy.wait()


def per_device(saved_input, upstream, weights):
    rows, cols, width = upstream.shape
    own_cols, channels = saved_input.shape[1], saved_input.shape[2]
    chunk = own_cols * rows
    x = jnp.transpose(saved_input, (1, 0, 2)).reshape(chunk, channels)
    hbm = pl.BlockSpec(memory_space=pl.ANY)
    vmem = pl.BlockSpec(memory_space=pltpu.VMEM)
    block = channels // 4
    gi_shape, gk_shape = (chunk, channels), (9, block, width)
    landing = []
    for _, _, n in CLASSES:
        for shape in ((2, 2, n), (2, NZ, n), (2, n // 2), (2, n)):
            landing.append(pltpu.VMEM((*shape, channels), BF16))
    gi, gk = pl.pallas_call(
        kernel,
        name="conv_backward",
        out_shape=(pltpu.VMEM(gi_shape, BF16), pltpu.VMEM(gk_shape, F32)),
        in_specs=[hbm, hbm, hbm],
        out_specs=(vmem, vmem),
        scratch_shapes=[
            pltpu.VMEM((rows, cols, width), BF16),
            pltpu.VMEM((channels, 9 * width), BF16),
            pltpu.VMEM(((rows + 2) * cols, width), F32),
            pltpu.VMEM((cols + 2, rows, 9 * width), BF16),
            pltpu.VMEM((NY, NZ, chunk, channels), BF16),
            pltpu.VMEM((NY, NZ, chunk, channels), BF16),
            pltpu.VMEM((4, block, 9 * width), F32),
            pltpu.VMEM((channels, NZ * chunk), BF16),
            pltpu.VMEM((4, block, 9 * width), BF16),
            pltpu.VMEM((2, block, 9 * width), BF16),
            pltpu.VMEM((block, 9 * width), BF16),
            pltpu.VMEM((block, 9 * width), BF16),
            pltpu.VMEM((2, cols, width), BF16),
            pltpu.SemaphoreType.DMA((1,)),
            pltpu.SemaphoreType.DMA((MESSAGES,)),
            pltpu.SemaphoreType.DMA((13,)),
            *landing,
        ],
        compiler_params=pltpu.CompilerParams(
            collective_id=0, has_side_effects=True, vmem_limit_bytes=56 * 1024 * 1024
        ),
    )(x, upstream, weights.reshape(9, channels, width))
    gi, gk = pl.pallas_call(
        write_out,
        name="write_out",
        out_shape=(jax.ShapeDtypeStruct(gi_shape, BF16), jax.ShapeDtypeStruct(gk_shape, F32)),
        in_specs=[vmem, vmem],
        out_specs=(hbm, hbm),
        scratch_shapes=[pltpu.SemaphoreType.DMA((2,))],
        compiler_params=pltpu.CompilerParams(vmem_limit_bytes=1024 * 1024),
    )(gi, gk)
    input_grad = jnp.transpose(gi.reshape(own_cols, rows, channels), (1, 0, 2))
    return input_grad, gk.reshape(3, 3, block, width)


def solution(mesh):
    placed = (P("tile", "filt", "chan"), P("tile", None, "filt"), P(None, None, "chan", "filt"))
    return jax.shard_map(
        per_device,
        mesh=mesh,
        in_specs=placed,
        out_specs=(P("tile", "filt", "chan"), P(None, None, ("chan", "tile"), "filt")),
        check_vma=False,
    )
```

time: 63.1 us -> 60.2 us (0.954)
  Pallas kernels: 62.3 us -> 59.5 us
    pallas_call x1, Pallas kernels: 61.4 us -> 58.6 us  [per_device(): pl.pallas_call(kernel, name='conv_backward', out_shape=(pltpu.VMEM(gi_sha...]
where the time goes in v4:
time: 60.2 us; the launch traced here: 60.1 us
  Pallas kernels  59.5 us (99%)
  between operations  0.64 us (1%)
    pallas_call x1, Pallas kernels, per_device(): pl.pallas_call(kernel, name='conv_backward', out_shape=(pltpu.VMEM(gi_sha...  58.6 us

profile of v4, /device:TPU:1, one launch (start us, length us, event | category | flops | bytes accessed | tf_op | source)
XLA Modules:
  0.0 60.1 jit_solution(3143231809660350576)
XLA Ops:
  0.6 58.6 %conv_backward.1 = (bf16[192,512]{1,0:T(8,128)(2,1)S(1)}, f32[9,128,128]{2,1,0:T(8,128)S(1)}) custom-call(bf16[192,512]{1,0:T(8,128)(2,1)} %bitcast.9, bf16[64,48,128]{2,1,0:T(8,128)(2,1)} %u_ref.1, bf16[9,512,128]{2,1,0:T(8,128)(2,1)} %bitcast.8), custom_call_target="tpu_custom_call" | custom-call | tf_op jit(solution)/shard_map/conv_backward/pallas_call | solution.py:439
  59.2 0.9 %write_out.1 = (bf16[192,512]{1,0:T(8,128)(2,1)}, f32[9,128,128]{2,1,0:T(8,128)}) custom-call(bf16[192,512]{1,0:T(8,128)(2,1)S(1)} %get-tuple-element.6.gi_ref, f32[9,128,128]{2,1,0:T(8,128)S(1)} %get-tuple-element.7.gk_ref), custom_call_target="tpu_custom_call" | custom-call | tf_op jit(solution)/shard_map/write_out/pallas_call | solution.py:468

commit v5 on v4

--- a/solution.py
+++ b/solution.py
@@ -18,22 +18,13 @@
 RELAY = {2: (UP, 0), 1: (UP, 1), 3: (DOWN, 0), 0: (DOWN, 1)}
 CLASSES = (("rz", "z", 64), ("ry", "y", 64), ("rw", "y", 64))
 W_PARTS = 3
-MESSAGES = 89
+MESSAGES = 58
 
 ORDER = (
-    "pass00", "pass10", "dgrad2", "ry_far00", "z2_1", "z2_0", "rw_far00",
-    "y1_011", "y1_130", "y1_030", "dgrad1", "y1_111", "dgrad0", "y1_031",
-    "y1_110", "y1_010", "dgrad3", "ry_far01", "rz_far01", "y1_131", "y1_121",
-    "rz_far00", "y1_020", "y1_120", "y1_021", "rz_far10", "rz_dir3", "pass03",
-    "pass11", "rz_dir2", "rz_dir0", "rz_far11", "pass12", "pass01", "pass13",
-    "pass02", "rz_dep2", "ry_dir2", "rz_dep3", "rz_dep0", "ry_dep2", "rw_dep2",
-    "rz_dep1", "rz_dir1", "rw_far10", "rw_dir2", "rw_far01", "ry_far10", "wgrad0",
-    "wgrad1", "wgrad3", "rw_dir1", "wgrad2_0", "wcore_0", "ry_far2", "ry_dir3",
-    "rw_far11", "wgrad2_1", "ry_dep3", "ry_far11", "rw_far2", "wcore_1", "wlo_0",
-    "rw_dep1", "wgrad2_2", "ry_dir1", "rw_dep3", "ry_dep1", "rw_dir3", "wlo_1",
-    "ry_near21", "rz_far2", "rw_near20", "wfin_0", "rw_dir0", "ry_near20", "wcore_2",
-    "rw_near21", "rz_near20", "rz_near21", "ry_dep0", "wlo_2", "ry_dir0", "rw_dep0",
-    "rz_fin", "ry_fin", "wfin_1", "rw_fin", "wfin_2",
+    8, 19, 5, 57, 7, 24, 13, 18, 6, 27, 16, 4, 3, 42, 45, 12, 41, 28, 23, 17, 14, 15, 26, 11,
+    20, 44, 25, 9, 47, 50, 49, 22, 51, 21, 0, 67, 48, 52, 10, 60, 1, 76, 68, 73, 58, 54, 74, 65,
+    2, 53, 29, 30, 81, 83, 71, 33, 70, 34, 61, 84, 31, 69, 66, 85, 55, 35, 82, 37, 38, 87, 86, 79,
+    39, 32, 77, 59, 62, 63, 78, 64, 43, 46, 36, 75, 80, 56, 72, 40, 88,
 )
 
 
@@ -74,8 +65,8 @@
     def at_z(direction):
         return {"filt": y * NZ + zed(NEAR[direction])}
 
-    def message(key, src, dst, peer, send_sem=None):
-        n = numbers.setdefault(key, len(numbers))
+    def message(key, src, dst, peer, send_sem=None, group=None):
+        n = numbers.setdefault(group or key, len(numbers))
 
         def make():
             return pltpu.make_async_remote_copy(
@@ -93,6 +84,11 @@
     def arrive(move):
         move.arrive()
 
+    def arrive_all(group, place):
+        if group not in landed:
+            landed.add(group)
+            pltpu.make_async_copy(place, place, rsem.at[numbers[group]]).wait()
+
     other_core = {"tile": lo * 2 + 1 - core}
     other_lo = {"tile": (1 - lo) * 2 + core}
     cross = {"tile": (1 - lo) * 2 + 1 - core}
@@ -102,19 +98,14 @@
     for peer in peers:
         pl.semaphore_signal(barrier, inc=1, device_id=peer, device_id_type=pl.DeviceIdType.MESH)
 
-    upstream_copy = pltpu.make_async_copy(u_ref, u_vm, lsem.at[10])
+    upstream_copy = pltpu.make_async_copy(u_ref, u_vm, lsem.at[1])
     upstream_copy.start()
-    own = pltpu.make_async_copy(x_ref, a_buf.at[0, z], lsem.at[9])
+    own = pltpu.make_async_copy(x_ref, a_buf.at[0, z], lsem.at[2])
     own.start()
-    weights = []
     for si in range(3):
         for ri in range(3):
-            place = si * 3 + ri
-            copy = pltpu.make_async_copy(
-                k_ref.at[ri * 3 + si], kc.at[:, pl.ds(place * width, width)], lsem.at[place]
-            )
-            copy.start()
-            weights.append(copy)
+            place = kc.at[:, pl.ds((si * 3 + ri) * width, width)]
+            pltpu.make_async_copy(k_ref.at[ri * 3 + si], place, lsem.at[0]).start()
     with mark("a_barrier"):
         pl.semaphore_wait(barrier, len(peers))
 
@@ -130,28 +121,28 @@
 
     def y1(d, b, h):
         src = x_ref.at[part(h)] if b == 0 else a_buf.at[0, zed(b), part(h)]
-        return message(("y1", d, b, h), src, a_buf.at[NEAR[1 - d], zed(b), part(h)], at_y(d))
+        place = a_buf.at[NEAR[1 - d], zed(b), part(h)]
+        return message(("y1", d, b, h), src, place, at_y(d), group=None if h == d else ("y1", d))
 
     def y2(d, b):
-        return message(
-            ("y2", d, b), a_buf.at[NEAR[1 - d], zed(b), part(d)], a_buf.at[2, zed(b), part(d)], at_y(d)
-        )
+        src, place = a_buf.at[NEAR[1 - d], zed(b), part(d)], a_buf.at[2, zed(b), part(d)]
+        return message(("y2", d, b), src, place, at_y(d), group=("y2",))
 
     def columns(p):
         return pl.ds(p * taps, taps)
 
     def wcore(k, p):
         src = wb.at[2 * k + 1 - core, :, columns(p)]
-        return message(("wc", k, p), src, wc_in.at[k, :, columns(p)], other_core)
+        return message(("wc", k, p), src, wc_in.at[k, :, columns(p)], other_core, group=("wc", p))
 
     def wlo(p):
         return message(("wz", p), wz_out.at[:, columns(p)], wz_in.at[:, columns(p)], other_lo)
 
     def halo_down():
-        return message(("halo", 0), u_ref.at[0], halo.at[1], {"tile": tile - 1}, lsem.at[11]).make()
+        return message(("halo", 0), u_ref.at[0], halo.at[1], {"tile": tile - 1}, lsem.at[3]).make()
 
     def halo_up():
-        return message(("halo", 1), u_ref.at[rows - 1], halo.at[0], {"tile": tile + 1}, lsem.at[12]).make()
+        return message(("halo", 1), u_ref.at[rows - 1], halo.at[0], {"tile": tile + 1}, lsem.at[4]).make()
 
     class Reduce:
         def __init__(self, name, ring, low, count, bufs):
@@ -174,7 +165,8 @@
 
         def near(self, d, b):
             src = p_buf.at[self.block(NEAR[d], b)]
-            return message((self.name, "near", d, b), src, self.near_in.at[d, b], self.first(d))
+            place, group = self.near_in.at[d, b], (self.name, "near", b)
+            return message((self.name, "near", d, b), src, place, self.first(d), group=group)
 
         def far2(self, d):
             src = p_buf.at[self.block(0, 2, d)]
@@ -182,7 +174,8 @@
 
         def near2(self, d):
             src = p_buf.at[self.block(0, NEAR[d])]
-            return message((self.name, "near2", d), src, self.near2_in.at[d], self.second(d))
+            place, group = self.near2_in.at[d], (self.name, "near2")
+            return message((self.name, "near2", d), src, place, self.second(d), group=group)
 
         def send_far(self, d, k):
             start(self.far(d, k))
@@ -198,8 +191,7 @@
             start(self.near(d, b))
 
         def near_sum(self, b):
-            for d in BOTH:
-                arrive(self.near(d, b))
+            arrive_all((self.name, "near", b), self.near_in.at[:, b])
             own_term = p_buf[self.block(0, b)].astype(F32)
             return own_term + self.near_in[UP, b].astype(F32) + self.near_in[DOWN, b].astype(F32)
 
@@ -220,8 +212,7 @@
 
         def finish(self):
             total = self.near_sum(0)
-            for d in BOTH:
-                arrive(self.near2(d))
+            arrive_all((self.name, "near2"), self.near2_in)
             total += self.near2_in[UP].astype(F32) + self.near2_in[DOWN].astype(F32)
             place = pl.ds(self.low, self.count)
             gi_ref[place] = jnp.where(a_buf[0, z, place] > 0, total, 0.0).astype(BF16)
@@ -280,8 +271,7 @@
                 for si in range(3):
                     s_buf[j + si, :, pl.ds(si * taps + ri * width, width)] = value
 
-        for copy in weights:
-            copy.wait()
+        pltpu.make_async_copy(kc, kc, lsem.at[0]).wait()
 
     def stacked(a, lanes=slice(None)):
         block = s_buf[pl.ds(ycoord(a) * group_cols + 1, group_cols), :, lanes]
@@ -316,15 +306,13 @@
 
     def wgrad_y(d):
         for b in range(NZ):
-            for h in BOTH:
-                arrive(y1(d, b, h))
+            arrive(y1(d, b, d))
+        arrive_all(("y1", d), a_buf.at[NEAR[1 - d], :, part(1 - d)])
         wgrad(NEAR[1 - d])
 
     def wgrad_last(p):
         if p == 0:
-            for b in range(NZ):
-                for d in BOTH:
-                    arrive(y2(d, b))
+            arrive_all(("y2",), a_buf.at[2])
             activate(2)
         value = jnp.dot(at[...], stacked(2, columns(p)), preferred_element_type=F32)
         wacc[:, :, columns(p)] += value.reshape(wacc.shape[0], wacc.shape[1], taps)
@@ -335,8 +323,7 @@
             start(wcore(k, p))
 
     def wlo_out(p):
-        for k in (0, 1):
-            arrive(wcore(k, p))
+        arrive_all(("wc", p), wc_in.at[:, :, columns(p)])
         total = wacc[2 * (1 - lo) + core, :, columns(p)] + wc_in[1 - lo, :, columns(p)].astype(F32)
         wz_out[:, columns(p)] = total.astype(BF16)
         start(wlo(p))
@@ -392,10 +379,12 @@
             steps[f"{name}_dep{b}"] = functools.partial(red.send_relayed, b)
         steps[f"{name}_far2"] = red.send_far2
         steps[f"{name}_fin"] = red.finish
-    assert set(ORDER) == set(steps) and len(ORDER) == len(steps)
-    for n, name in enumerate(ORDER):
+    listed = list(steps.items())
+    assert sorted(ORDER) == list(range(len(listed)))
+    for n, place in enumerate(ORDER):
+        name, step = listed[place]
         with mark(f"{n:03}_{name}"):
-            steps[name]()
+            step()
     assert len(numbers) == MESSAGES
     with mark("y_sends"):
         column = rows * 9 * width * 2
@@ -458,7 +447,7 @@
             pltpu.VMEM((2, cols, width), BF16),
             pltpu.SemaphoreType.DMA((1,)),
             pltpu.SemaphoreType.DMA((MESSAGES,)),
-            pltpu.SemaphoreType.DMA((13,)),
+            pltpu.SemaphoreType.DMA((5,)),
             *landing,
         ],
         compiler_params=pltpu.CompilerParams(

time: 60.2 us -> 59.5 us (0.988)
  Pallas kernels: 59.5 us -> 58.8 us
    pallas_call x1, Pallas kernels: 58.6 us -> 57.9 us  [per_device(): pl.pallas_call(kernel, name='conv_backward', out_shape=(pltpu.VMEM(gi_sha...]
where the time goes in v5:
time: 59.5 us; the launch traced here: 59.4 us
  Pallas kernels  58.8 us (99%)
  between operations  0.64 us (1%)
    pallas_call x1, Pallas kernels, per_device(): pl.pallas_call(kernel, name='conv_backward', out_shape=(pltpu.VMEM(gi_sha...  57.9 us

profile of v5, /device:TPU:1, one launch (start us, length us, event | category | flops | bytes accessed | tf_op | source)
XLA Modules:
  0.0 59.4 jit_solution(4040210012386598854)
XLA Ops:
  0.6 57.9 %conv_backward.1 = (bf16[192,512]{1,0:T(8,128)(2,1)S(1)}, f32[9,128,128]{2,1,0:T(8,128)S(1)}) custom-call(bf16[192,512]{1,0:T(8,128)(2,1)} %bitcast.9, bf16[64,48,128]{2,1,0:T(8,128)(2,1)} %u_ref.1, bf16[9,512,128]{2,1,0:T(8,128)(2,1)} %bitcast.8), custom_call_target="tpu_custom_call" | custom-call | tf_op jit(solution)/shard_map/conv_backward/pallas_call | solution.py:428
  58.5 0.9 %write_out.1 = (bf16[192,512]{1,0:T(8,128)(2,1)}, f32[9,128,128]{2,1,0:T(8,128)}) custom-call(bf16[192,512]{1,0:T(8,128)(2,1)S(1)} %get-tuple-element.6.gi_ref, f32[9,128,128]{2,1,0:T(8,128)S(1)} %get-tuple-element.7.gk_ref), custom_call_target="tpu_custom_call" | custom-call | tf_op jit(solution)/shard_map/write_out/pallas_call | solution.py:457

commit v6 on v5

--- a/solution.py
+++ b/solution.py
@@ -106,6 +106,8 @@
         for ri in range(3):
             place = kc.at[:, pl.ds((si * 3 + ri) * width, width)]
             pltpu.make_async_copy(k_ref.at[ri * 3 + si], place, lsem.at[0]).start()
+    s_buf[1, :, 2 * taps :] = jnp.zeros((rows, taps), BF16)
+    s_buf[cols, :, :taps] = jnp.zeros((rows, taps), BF16)
     with mark("a_barrier"):
         pl.semaphore_wait(barrier, len(peers))
 
@@ -230,6 +232,7 @@
     for h in BOTH:
         for d in BOTH:
             start(z1(d, h ^ d))
+        for d in BOTH:
             start(y1(d, 0, h ^ d))
 
     with mark("b_uf"):
@@ -239,8 +242,6 @@
         def _(i):
             uf[pl.ds(pl.multiple_of((i + 1) * cols, 8), cols), :] = u_vm[i].astype(F32)
 
-    s_buf[1, :, 2 * taps :] = jnp.zeros((rows, taps), BF16)
-    s_buf[cols, :, :taps] = jnp.zeros((rows, taps), BF16)
     bottom = (rows + 1) * cols
     with mark("c_halo"):
 

time: 59.5 us -> 59.5 us (level)
  no operation moved by 1% of the time
where the time goes in v6:
time: 59.5 us; the launch traced here: 59.4 us
  Pallas kernels  58.8 us (99%)
  between operations  0.64 us (1%)
    pallas_call x1, Pallas kernels, per_device(): pl.pallas_call(kernel, name='conv_backward', out_shape=(pltpu.VMEM(gi_sha...  57.9 us

profile of v6, /device:TPU:1, one launch (start us, length us, event | category | flops | bytes accessed | tf_op | source)
XLA Modules:
  0.0 59.4 jit_solution(4447204832002826358)
XLA Ops:
  0.6 57.9 %conv_backward.1 = (bf16[192,512]{1,0:T(8,128)(2,1)S(1)}, f32[9,128,128]{2,1,0:T(8,128)S(1)}) custom-call(bf16[192,512]{1,0:T(8,128)(2,1)} %bitcast.9, bf16[64,48,128]{2,1,0:T(8,128)(2,1)} %u_ref.1, bf16[9,512,128]{2,1,0:T(8,128)(2,1)} %bitcast.8), custom_call_target="tpu_custom_call" | custom-call | tf_op jit(solution)/shard_map/conv_backward/pallas_call | solution.py:429
  58.5 0.9 %write_out.1 = (bf16[192,512]{1,0:T(8,128)(2,1)}, f32[9,128,128]{2,1,0:T(8,128)}) custom-call(bf16[192,512]{1,0:T(8,128)(2,1)S(1)} %get-tuple-element.6.gi_ref, f32[9,128,128]{2,1,0:T(8,128)S(1)} %get-tuple-element.7.gk_ref), custom_call_target="tpu_custom_call" | custom-call | tf_op jit(solution)/shard_map/write_out/pallas_call | solution.py:458
